TPU v7x, 32 devices: a whole 2x2x4 slice. The times are simulated.
32 devices in a mesh: dp: 4 (over y, x), shard: 8 (over z, core).
Axes of the slice: x: 2, y: 2, z: 4, core: 2. Of those that a mesh axis runs over, the one named last changes fastest.
Arguments:
- id_table: float32 [262144, 128], P(('dp', 'shard')), may hold values from -6 to 6
- ada_state: float32 [262144], P(('dp', 'shard')), may hold values from 0.01 to 1
- user_first: float32 [128, 512], replicated, may hold values from -0.5 to 0.5
- user_second: float32 [512, 128], replicated, may hold values from -0.25 to 0.25
- item_first: float32 [128, 512], replicated, may hold values from -0.5 to 0.5
- item_second: float32 [512, 128], replicated, may hold values from -0.25 to 0.25
- fetch_rows: int32 [32, 4, 8, 72], P(('dp', 'shard')), may hold values from 0 to 8191
- lookup_slots: int32 [32, 1536], P(('dp', 'shard')), may hold values from 0 to 2303
Outputs:
- new_table: float32 [262144, 128], P(('dp', 'shard'))
- new_state: float32 [262144], P(('dp', 'shard'))
- user_first_grad: float32 [128, 512], replicated
- user_second_grad: float32 [512, 128], replicated
- item_first_grad: float32 [128, 512], replicated
- item_second_grad: float32 [512, 128], replicated
- mean_loss: float32 [], replicated
All inputs are finite; a program needn't handle non-finite values.
Results may differ from a plain program's by a relative error of at most 0.0038.
The roundings to bfloat16 on the way count: a program that leaves them out, or rounds other values in their place, can miss the bound.
Values may be sent and summed in bfloat16 or wider, within the bound.
No kernel may reach another device: no remote copies, remote signals or barrier semaphores. Data moves between devices by JAX's collectives and lax.ppermute only.
A program may use at most 128 MiB of HBM per device.

v0:
```python
import jax
import jax.numpy as jnp
from jax import lax
from jax.sharding import PartitionSpec as P

EXAMPLES_ON_CHIP = 512


highest = lax.Precision.HIGHEST
logit_divisor = 0.025
learn_rate = 0.1
epsilon = 1e-08


def tower_pass(looked, first_w, second_w):
    hidden_act = jax.nn.silu(
        jnp.dot(looked, first_w, precision=highest, preferred_element_type=jnp.float32)
    )
    tower_out = jnp.dot(hidden_act, second_w, precision=highest, preferred_element_type=jnp.float32)
    return tower_out / jnp.sqrt(jnp.sum(tower_out * tower_out, axis=1, keepdims=True) + 1e-06)


def score_block(user_half_precision, candidate_half_precision):
    return (
        jnp.dot(user_half_precision, candidate_half_precision.T, preferred_element_type=jnp.float32)
        / logit_divisor
    )


def cand_step(candidate_half_precision, user_half_precision):
    exponent = jnp.exp(score_block(user_half_precision, candidate_half_precision))
    collected_entries = jnp.dot(
        exponent.astype(jnp.bfloat16), candidate_half_precision, preferred_element_type=jnp.float32
    )
    return (jnp.sum(exponent, axis=1), collected_entries)


def item_term(user_half_precision, log_z, candidate_half_precision):
    softmax = jnp.exp(
        score_block(user_half_precision, candidate_half_precision) - log_z[:, None]
    ).astype(jnp.bfloat16)
    return jnp.dot(softmax.T, user_half_precision, preferred_element_type=jnp.float32)


def per_device(
    id_table, ada_state, user_first, user_second, item_first, item_second, fetch_rows, lookup_slots
):
    target_index_vector = id_table.shape[1]
    examples_on_chip = EXAMPLES_ON_CHIP
    asked_rows = lax.all_to_all(
        lax.all_to_all(fetch_rows[0], "dp", split_axis=0, concat_axis=0, tiled=True),
        "shard",
        split_axis=1,
        concat_axis=1,
        tiled=True,
    )
    fetched = jnp.take(id_table, asked_rows.reshape(-1), axis=0).reshape(
        asked_rows.shape + (target_index_vector,)
    )
    returned = lax.all_to_all(
        lax.all_to_all(fetched, "dp", split_axis=0, concat_axis=0, tiled=True),
        "shard",
        split_axis=1,
        concat_axis=1,
        tiled=True,
    )
    slot_rows = returned.reshape(-1, target_index_vector)
    slot_index = lookup_slots[0]
    looked = jnp.take(slot_rows, slot_index, axis=0)
    user_vec, user_pull = jax.vjp(tower_pass, looked[:examples_on_chip], user_first, user_second)
    item_vec, item_pull = jax.vjp(tower_pass, looked[examples_on_chip:], item_first, item_second)
    user_half_precision = user_vec.astype(jnp.bfloat16)
    item_bf = item_vec.astype(jnp.bfloat16)
    query_single_float = user_half_precision.astype(jnp.float32)
    resident_target_entries = item_bf[:examples_on_chip].astype(jnp.float32)
    matching_pair_logit = (
        jnp.sum(query_single_float * resident_target_entries, axis=1) / logit_divisor
    )
    reduced_aggregates, collected_entries = cand_step(
        lax.all_gather(item_bf, "dp", axis=0, tiled=True), user_half_precision
    )
    log_z = jnp.log(reduced_aggregates)
    target_derivative_accrual = item_term(
        lax.all_gather(user_vec, "dp", axis=0, tiled=True).astype(jnp.bfloat16),
        lax.all_gather(log_z, "dp", axis=0, tiled=True),
        item_bf,
    )
    query_adjoint = (
        collected_entries / reduced_aggregates[:, None] - resident_target_entries
    ) / logit_divisor
    target_adjoint = (
        target_derivative_accrual.at[:examples_on_chip].add(-query_single_float) / logit_divisor
    )
    user_look, user_first_g, user_second_g = user_pull(query_adjoint)
    item_look, item_first_g, item_second_g = item_pull(target_adjoint)
    look_grads = jnp.concatenate([user_look, item_look], axis=0)
    slot_grads = jnp.zeros_like(slot_rows).at[slot_index].add(look_grads)
    sent_back = lax.all_to_all(
        lax.all_to_all(
            slot_grads.reshape(returned.shape).astype(jnp.bfloat16),
            "dp",
            split_axis=0,
            concat_axis=0,
            tiled=True,
        ),
        "shard",
        split_axis=1,
        concat_axis=1,
        tiled=True,
    ).astype(jnp.float32)
    grad_rows = (
        jnp.zeros_like(id_table)
        .at[asked_rows.reshape(-1)]
        .add(sent_back.reshape(-1, target_index_vector))
    )
    new_state = ada_state + jnp.mean(grad_rows * grad_rows, axis=1)
    new_table = id_table - learn_rate * grad_rows / (jnp.sqrt(new_state)[:, None] + epsilon)
    loss_part = jnp.sum(log_z - matching_pair_logit)
    summed = lax.psum(
        (user_first_g, user_second_g, item_first_g, item_second_g, loss_part), ("dp", "shard")
    )
    shard_number = lax.axis_size("dp") * lax.axis_size("shard")
    return (
        new_table,
        new_state,
        summed[0] / shard_number,
        summed[1] / shard_number,
        summed[2] / shard_number,
        summed[3] / shard_number,
        summed[4] / (shard_number * examples_on_chip),
    )


def solution(mesh):
    return jax.shard_map(
        per_device,
        mesh=mesh,
        in_specs=(
            P(("dp", "shard"), None),
            P(("dp", "shard")),
            P(),
            P(),
            P(),
            P(),
            P(("dp", "shard"), None, None, None),
            P(("dp", "shard"), None),
        ),
        out_specs=(P(("dp", "shard"), None), P(("dp", "shard")), P(), P(), P(), P(), P()),
        check_vma=False,
    )
```

profile of v0, /device:TPU:0, one launch (start us, length us, event | category | flops | bytes accessed | tf_op | source)
XLA Modules:
  0.0 361.9 jit_solution(15782953325688524731)
XLA Ops:
  7.2 10.0 %all_to_all.30 = s32[4,8,72]{2,1,0:T(8,128)S(1)} all-to-all(s32[4,8,72]{2,1,0:T(8,128)} %bitcast.34), channel_id=1, replica_groups=mesh['dp'=4,'shard'=8] {'dp'}, dimensions={0} | all-to-all | bytes 18432 | tf_op jit(solution)/shard_map/all_to_all | solution.py:51
  17.2 10.3 %all_to_all.31 = s32[4,8,72]{2,0,1:T(4,128)S(1)} all-to-all(s32[4,8,72]{2,0,1:T(4,128)S(1)} %copy.24), channel_id=1, replica_groups=mesh['dp'=4,'shard'=8] {'shard'}, dimensions={1} | all-to-all | bytes 18432 | tf_op jit(solution)/shard_map/all_to_all | solution.py:50
  28.3 6.1 %gather_fusion = f32[2304,128]{1,0:T(8,128)S(1)} fusion(f32[8192,128]{1,0:T(8,128)} %param.10, s32[3072]{0:T(1024)S(1)} %pad_clamp_fusion), kind=kCustom, calls=%fused_computation | custom fusion | bytes 2368512 | tf_op jit(solution)/shard_map/jit(_take)/gather | solution.py:57
  34.9 18.2 %all_to_all.32 = f32[4,8,72,128]{3,2,1,0:T(8,128)S(1)} all-to-all(f32[4,8,72,128]{3,2,1,0:T(8,128)S(1)} %broadcast_select_fusion), channel_id=1, replica_groups=mesh['dp'=4,'shard'=8] {'dp'}, dimensions={0} | all-to-all | bytes 2359296 | tf_op jit(solution)/shard_map/all_to_all | solution.py:61
  54.2 3.6 all-to-all-start.3
  57.9 29.1 %all-to-all-done.3 = f32[4,8,72,128]{3,2,0,1:T(8,128)S(1)} async-done(((f32[4,8,72,128]{3,2,0,1:T(8,128)}), f32[4,8,72,128]{3,2,0,1:T(8,128)S(1)}, u32[]{:S(2)}, u32[]{:S(2)}) %all-to-all-start.3) | async-done | bytes 1179680 | tf_op jit(solution)/shard_map/all_to_all | solution.py:60
  91.9 2.7 multiply_reduce_fusion.2
  97.3 2.7 multiply_reduce_fusion.4
  101.3 11.5 %all_gather.10 = bf16[2048,128]{0,1:T(8,128)(2,1)} all-gather(bf16[512,128]{0,1:T(8,128)(2,1)S(1)} %get-tuple-element.24), channel_id=1, replica_groups=mesh['dp'=4,'shard'=8] {'dp'}, dimensions={0}, use_global_device_ids=true | all-gather | bytes 655360 | tf_op jit(solution)/shard_map/all_gather | solution.py:84
  112.8 8.4 %all-gather.3.cloned.1.call-done = bf16[4096,128]{0,1:T(8,128)(2,1)} async-done(((bf16[1024,128]{0,1:T(8,128)(2,1)}), bf16[4096,128]{0,1:T(8,128)(2,1)}) %all-gather.3.cloned.1.call-update) | async-done | bytes 1048592 | tf_op jit(solution)/shard_map/all_gather | solution.py:80
  121.2 5.8 %fusion = (f32[512]{0:T(512)S(1)}, f32[512,4096]{1,0:T(8,128)}) fusion(bf16[512,128]{0,1:T(8,128)(2,1)S(1)} %get-tuple-element.24, bf16[4096,128]{0,1:T(8,128)(2,1)} %all-gather.3.cloned.1.call-done), kind=kOutput, calls=%fused_computation.6 | convolution fusion | flops 541064704 | bytes 9570304 | tf_op jit(solution)/shard_map/dot_general | solution.py:25
  127.6 8.8 %all-gather = f32[4,1,512]{2,1,0:T(1,128)} all-gather(f32[1,1,512]{2,1,0:T(1,128)S(1)} %bitcast.36), channel_id=1, replica_groups=mesh['dp'=4,'shard'=8] {'dp'}, dimensions={0}, use_global_device_ids=true | all-gather | bytes 10240 | tf_op jit(solution)/shard_map/all_gather | solution.py:85
  136.5 4.1 %fusion.10 = f32[1024,128]{0,1:T(8,128)} fusion(bf16[1024,128]{0,1:T(8,128)(2,1)S(1)} %copy-done.3, f32[2048]{0:T(1024)} %bitcast.35, bf16[2048,128]{0,1:T(8,128)(2,1)} %all_gather.10), kind=kOutput, calls=%fused_computation.19 | convolution fusion | flops 1080033280 | bytes 1318912 | tf_op jit(solution)/shard_map/dot_general | solution.py:42
  144.6 3.8 %fusion.6 = f32[1024,512]{1,0:T(8,128)S(1)} fusion(f32[1024,512]{1,0:T(8,128)S(1)} %fusion.30, f32[512,128]{1,0:T(8,128)S(1)} %copy-done, f32[1024,128]{0,1:T(8,128)} %copy-done.5, f32[1024,128]{0,1:T(8,128)} %fusion.37, f32[1024]{0:T(1024)S(1)} %multiply_multiply_fusion, f32[1024]{0:T(1024)} %copy-done.17), kind=kOutput, calls=%fused_computation.14 | convolution fusion | flops 810680320 | bytes 5513216 | tf_op jit(solution)/shard_map/transpose(jvp())/dot_general | solution.py:19
  154.8 2.6 fusion.43
  160.0 9.3 %scatter_custom_fusion = f32[2304,128]{1,0:T(8,128)S(1)} fusion(s32[1536]{0:T(1024)S(1)} %fusion.48, f32[1024,128]{1,0:T(8,128)} %fusion.58, f32[]{:T(128)} %constant.111, f32[512,128]{1,0:T(8,128)S(1)} %fusion.57, f32[]{:T(128)} %constant.90.clone.1), kind=kCustom, calls=%fused_computation.28 | custom fusion | flops 393216 | bytes 1966088 | tf_op jit(solution)/shard_map/scatter-add | solution.py:97
  170.2 3.5 all-to-all-start.4
  173.7 6.2 %fusion.32 = f32[512,128]{1,0:T(8,128)} fusion(f32[1024,512]{1,0:T(8,128)} %copy-done.4, f32[1024,128]{0,1:T(8,128)} %copy-done.5, f32[1024,128]{0,1:T(8,128)} %fusion.37, f32[1024]{0:T(1024)S(1)} %copy-done.26, f32[1024]{0:T(1024)S(1)} %copy-done.18), kind=kOutput, calls=%fused_computation.45 | convolution fusion | flops 808058880 | bytes 3416064 | tf_op jit(solution)/shard_map/transpose(jvp())/dot_general | solution.py:19
  181.5 4.6 %all-to-all-start.5 = ((bf16[4,8,72,128]{3,2,0,1:T(8,128)(2,1)}), bf16[4,8,72,128]{3,2,0,1:T(8,128)(2,1)S(1)}, u32[]{:S(2)}, u32[]{:S(2)}) async-start(bf16[4,8,72,128]{3,2,0,1:T(8,128)(2,1)} %copy.29), calls=%async_computation.5 | async-start | bytes 1179648 | tf_op jit(solution)/shard_map/all_to_all | solution.py:98
  187.7 40.8 %psum.39 = f32[]{:T(128)} all-reduce(f32[]{:T(128)} %get-tuple-element.29), channel_id=1, replica_groups=mesh['dp'=4,'shard'=8] {'dp','shard'}, use_global_device_ids=true, to_apply=%region_14.15 | all-reduce | flops 1 | bytes 8 | tf_op jit(solution)/shard_map/psum | solution.py:119
  229.1 96.8 %all-reduce.3.cloned.1.call-done = (f32[128,512]{1,0:T(8,128)}, f32[512,128]{1,0:T(8,128)}, f32[128,512]{1,0:T(8,128)}, f32[512,128]{1,0:T(8,128)}) async-done(((f32[128,512]{1,0:T(8,128)}, f32[512,128]{1,0:T(8,128)}, f32[128,512]{1,0:T(8,128)}, f32[512,128]{1,0:T(8,128)}), (f32[128,512]{1,0:T(8,128)}, f32[512,128]{1,0:T(8,128)}, f32[128,512]{1,0:T(8,128)}, ...) | async-done | bytes 1048592 | tf_op jit(solution)/shard_map/psum | solution.py:119
  329.8 15.8 %scatter_custom_fusion.1 = f32[8192,128]{1,0:T(8,128)} fusion(s32[2304]{0:T(1024)} %copy-done.14, f32[]{:T(128)} %constant.90.clone.1, bf16[2304,128]{1,0:T(8,128)(2,1)S(1)} %bitcast.32), kind=kCustom, calls=%fused_computation.17 | custom fusion | flops 589824 | bytes 4784640 | tf_op jit(solution)/shard_map/scatter-add | solution.py:114
  345.6 3.5 multiply_reduce_fusion
  349.7 4.2 %divide_subtract_fusion = f32[8192,128]{1,0:T(8,128)} fusion(f32[8192,128]{1,0:T(8,128)S(1)} %copy-done.1, f32[8192,128]{1,0:T(8,128)} %scatter_custom_fusion.1, f32[8192]{0:T(1024)S(1)} %get-tuple-element.25), kind=kLoop, calls=%fused_computation.9 | loop fusion | flops 3145728 | bytes 12615680 | tf_op jit(solution)/shard_map/sub | solution.py:117
  (106 shorter events, 32.9 us)
Async XLA Ops:
  7.2 84.7 %copy-start = (f32[512,128]{1,0:T(8,128)S(1)}, f32[512,128]{1,0:T(8,128)}, u32[]{:S(2)}) copy-start(f32[512,128]{1,0:T(8,128)} %param.15) | copy-start | bytes 786436
  53.1 4.7 %copy-start.16 = (s32[1,1536]{1,0:T(1,128)S(1)}, s32[1,1536]{1,0:T(1,128)}, u32[]{:S(2)}) copy-start(s32[1,1536]{1,0:T(1,128)} %param.17) | copy-start | bytes 18436
  54.2 32.9 %all-to-all-start.3 = ((f32[4,8,72,128]{3,2,0,1:T(8,128)}), f32[4,8,72,128]{3,2,0,1:T(8,128)S(1)}, u32[]{:S(2)}, u32[]{:S(2)}) async-start(f32[4,8,72,128]{3,2,0,1:T(8,128)} %copy.27), calls=%async_computation.3 | async-start | bytes 2359296 | tf_op jit(solution)/shard_map/all_to_all | solution.py:60
  57.8 63.4 %all-gather.3.cloned.1.call-start = ((), (), s32[]{:S(2)}) async-start(), calls=%async_computation.6 | async-start | bytes 1310720 | tf_op jit(solution)/shard_map/all_gather | solution.py:80
  87.2 2.9 copy-start.12
  91.9 52.7 %copy-start.4 = (f32[1024,512]{1,0:T(8,128)}, f32[1024,512]{1,0:T(8,128)S(1)}, u32[]{:S(2)}) copy-start(f32[1024,512]{1,0:T(8,128)S(1)} %fusion.30) | copy-start | bytes 6291460
  91.9 4.3 %copy-start.10 = (f32[128,512]{1,0:T(8,128)S(1)}, f32[128,512]{1,0:T(8,128)}, u32[]{:S(2)}) copy-start(f32[128,512]{1,0:T(8,128)} %param.12) | copy-start | bytes 786436
  94.7 5.3 %copy-start.19 = (f32[1024]{0:T(1024)}, f32[1024]{0:T(1024)S(1)}, u32[]{:S(2)}) copy-start(f32[1024]{0:T(1024)S(1)} %get-tuple-element.33) | copy-start | bytes 12292
  95.4 4.6 %copy-start.17 = (f32[1024]{0:T(1024)}, f32[1024]{0:T(1024)S(1)}, u32[]{:S(2)}) copy-start(f32[1024]{0:T(1024)S(1)} %get-tuple-element.28) | copy-start | bytes 12292
  97.2 2.7 copy-start.8
  97.2 3.4 copy-start.3
  100.0 12.9 %copy-start.20 = (f32[512]{0:T(512)}, f32[512]{0:T(512)S(1)}, u32[]{:S(2)}) copy-start(f32[512]{0:T(512)S(1)} %get-tuple-element.32) | copy-start | bytes 6148
  121.2 5.8 %copy-start.22 = (f32[512]{0:T(512)S(1)}, f32[512]{0:T(512)}, u32[]{:S(2)}) copy-start(f32[512]{0:T(512)} %get-tuple-element.23) | copy-start | bytes 6148
  142.3 10.8 %slice-start = ((s8[8388608]{0:T(1024)(128)(4,1)}), s8[4194304]{0:T(1024)(128)(4,1)S(1)}, s32[]{:S(2)}) async-start(s8[8388608]{0:T(1024)(128)(4,1)} %bitcast.28), calls=%async_computation.8 | async-start | bytes 8388608
  144.6 3.8 %copy-start.25 = (f32[1024]{0:T(1024)}, f32[1024]{0:T(1024)S(1)}, u32[]{:S(2)}) copy-start(f32[1024]{0:T(1024)S(1)} %multiply_multiply_fusion) | copy-start | bytes 12292
  144.6 8.5 %slice-start.1 = ((s8[8388608]{0:T(1024)(128)(4,1)}), s8[4194304]{0:T(1024)(128)(4,1)S(1)}, s32[]{:S(2)}) async-start(s8[8388608]{0:T(1024)(128)(4,1)} %bitcast.28), calls=%async_computation.9 | async-start | bytes 8388608
  154.8 2.6 copy-start.27
  160.0 13.7 %copy-start.18 = (f32[1024]{0:T(1024)S(1)}, f32[1024]{0:T(1024)}, u32[]{:S(2)}) copy-start(f32[1024]{0:T(1024)} %copy-done.17) | copy-start | bytes 12292
  160.0 13.7 %copy-start.26 = (f32[1024]{0:T(1024)S(1)}, f32[1024]{0:T(1024)}, u32[]{:S(2)}) copy-start(f32[1024]{0:T(1024)} %copy-done.25) | copy-start | bytes 12292
  170.2 10.4 %all-to-all-start.4 = ((bf16[4,8,72,128]{3,2,1,0:T(8,128)(2,1)}), bf16[4,8,72,128]{3,2,1,0:T(8,128)(2,1)S(1)}, u32[]{:S(2)}, u32[]{:S(2)}) async-start(bf16[4,8,72,128]{3,2,1,0:T(8,128)(2,1)} %bitcast.33), calls=%async_computation.4 | async-start | bytes 1179648 | tf_op jit(solution)/shard_map/all_to_all | solution.py:99
  181.5 148.2 %all-to-all-start.5 = ((bf16[4,8,72,128]{3,2,0,1:T(8,128)(2,1)}), bf16[4,8,72,128]{3,2,0,1:T(8,128)(2,1)S(1)}, u32[]{:S(2)}, u32[]{:S(2)}) async-start(bf16[4,8,72,128]{3,2,0,1:T(8,128)(2,1)} %copy.29), calls=%async_computation.5 | async-start | bytes 1179648 | tf_op jit(solution)/shard_map/all_to_all | solution.py:98
  186.1 139.9 %all-reduce.3.cloned.1.call-start = ((), (), s32[]{:S(2)}) async-start(), calls=%async_computation.7 | async-start | bytes 2097152 | tf_op jit(solution)/shard_map/psum | solution.py:119
  345.6 3.5 copy-start.15
  345.6 4.1 %copy-start.1 = (f32[8192,128]{1,0:T(8,128)S(1)}, f32[8192,128]{1,0:T(8,128)}, u32[]{:S(2)}) copy-start(f32[8192,128]{1,0:T(8,128)} %param.10) | copy-start | bytes 12582916
  (11 other events, 16.5 us)
Sparse Core Ops, SparseCore 0:
  96.4 24.8 all-gather.2
  193.0 132.9 all-reduce.2
where the time goes:
time: 363 us; the launch traced here: 362 us
  waiting for transfers between devices  135 us (37%)
  blocking collectives  99.8 us (27%)
  other arithmetic  45.6 us (13%)
  matrix products  41 us (11%)
  between operations  16.3 us (4%)
  local copies, waits for them, and re-layouts  12.4 us (3%)
  starting transfers between devices  11.7 us (3%)
    psum x1, waiting for transfers between devices, per_device(): lax.psum((user_first_g, user_second_g, item_first_g, item_second_g, loss_...  96.8 us
    psum x1, blocking collectives, per_device(): lax.psum((user_first_g, user_second_g, item_first_g, item_second_g, loss_...  40.8 us
    all_to_all x1, waiting for transfers between devices, per_device(): lax.all_to_all(lax.all_to_all(fetched, 'dp', split_axis=0, concat_axis=0,...  29.1 us
    dot_general x6, matrix products, tower_pass(): jnp.dot(hidden_act, second_w, precision=highest, preferred_element_type=j...  19.6 us
    all_to_all x1, blocking collectives, per_device(): lax.all_to_all(fetched, 'dp', split_axis=0, concat_axis=0, tiled=True)  18.2 us
    scatter-add x1, other arithmetic, per_device(): grad_rows = jnp.zeros_like(id_table).at[asked_rows.reshape(-1)].add(sent_...  15.8 us
    all_gather x1, blocking collectives, per_device(): lax.all_gather(user_vec, 'dp', axis=0, tiled=True).astype(jnp.bfloat16)  11.5 us
    all_to_all x1, blocking collectives, per_device(): lax.all_to_all(lax.all_to_all(fetch_rows[0], 'dp', split_axis=0, concat_a...  10.3 us
  transfers between devices with their start and end apart: 5, of which 4 were waited for; matrix products, arithmetic and copies ran while one was open for 4% of the time, Pallas kernels for 0%

commit v1 on v0

v1 whole, which is shorter than its diff:
```python
import jax
import jax.numpy as jnp
from jax import lax
from jax.sharding import PartitionSpec as P

EXAMPLES_ON_CHIP = 512
AXES = ("dp", "shard")

highest = lax.Precision.HIGHEST
logit_divisor = 0.025
learn_rate = 0.1
epsilon = 1e-08


def tower_pass(looked, first_w, second_w):
    hidden_act = jax.nn.silu(
        jnp.dot(looked, first_w, precision=highest, preferred_element_type=jnp.float32)
    )
    tower_out = jnp.dot(hidden_act, second_w, precision=highest, preferred_element_type=jnp.float32)
    return tower_out / jnp.sqrt(jnp.sum(tower_out * tower_out, axis=1, keepdims=True) + 1e-06)


def exchange(x):
    return lax.all_to_all(x, AXES, split_axis=0, concat_axis=0, tiled=True)


def from_peers(blocks, n):
    out = [blocks[0]]
    for k in range(1, n):
        out.append(lax.ppermute(blocks[k], "dp", [(i, (i + k) % n) for i in range(n)]))
    return out


def to_owners(blocks, n):
    out = [blocks[0]]
    for k in range(1, n):
        out.append(lax.ppermute(blocks[k], "dp", [(i, (i - k) % n) for i in range(n)]))
    return out


def per_device(
    id_table, ada_state, user_first, user_second, item_first, item_second, fetch_rows, lookup_slots
):
    width = id_table.shape[1]
    n_dp = lax.axis_size("dp")
    n_all = n_dp * lax.axis_size("shard")
    cap = fetch_rows.shape[-1]
    n_ex = EXAMPLES_ON_CHIP
    asked = exchange(fetch_rows.reshape(n_all, cap))
    fetched = id_table.at[asked.reshape(-1)].get(mode="promise_in_bounds")
    slot_rows = exchange(fetched.reshape(n_all, cap, width)).reshape(-1, width)
    slot_index = lookup_slots[0]
    looked = slot_rows.at[slot_index].get(mode="promise_in_bounds")

    user_vec, user_pull = jax.vjp(tower_pass, looked[:n_ex], user_first, user_second)
    user_bf = user_vec.astype(jnp.bfloat16)
    group_users = from_peers([user_bf] * n_dp, n_dp)
    item_vec, item_pull = jax.vjp(tower_pass, looked[n_ex:], item_first, item_second)
    item_bf = item_vec.astype(jnp.bfloat16)

    parts, pulls, expos = [], [], []
    for block in group_users:
        expo = jnp.exp(
            jnp.dot(block, item_bf.T, preferred_element_type=jnp.float32) / logit_divisor
        )
        parts.append(jnp.sum(expo, axis=1))
        pulls.append(
            jnp.dot(expo.astype(jnp.bfloat16), item_bf, preferred_element_type=jnp.float32)
        )
        expos.append(expo)
    mine = jnp.stack(parts)
    seen = from_peers([mine] * n_dp, n_dp)
    totals = [sum(seen[k][(b - k) % n_dp] for k in range(n_dp)) for b in range(n_dp)]
    returned = to_owners([pulls[0]] + [p.astype(jnp.bfloat16) for p in pulls[1:]], n_dp)

    item_sum = sum(
        jnp.dot(
            (expo / total[:, None]).astype(jnp.bfloat16).T,
            block,
            preferred_element_type=jnp.float32,
        )
        for expo, total, block in zip(expos, totals, group_users)
    )
    user_f = user_bf.astype(jnp.float32)
    positive = item_bf[:n_ex].astype(jnp.float32)
    item_cot = (
        jnp.concatenate([item_sum[:n_ex] - user_f, item_sum[n_ex:]], axis=0) / logit_divisor
    )
    item_look, item_first_g, item_second_g = item_pull(item_cot)
    pulled = sum(p.astype(jnp.float32) for p in returned)
    user_cot = (pulled / totals[0][:, None] - positive) / logit_divisor
    user_look, user_first_g, user_second_g = user_pull(user_cot)
    pos_score = jnp.sum(user_f * positive, axis=1) / logit_divisor
    loss_part = jnp.sum(jnp.log(totals[0]) - pos_score)

    look_grads = jnp.concatenate([user_look, item_look], axis=0)
    slot_grads = jnp.zeros_like(slot_rows).at[slot_index].add(look_grads, mode="promise_in_bounds")
    weight_g = jnp.concatenate(
        [g.reshape(n_all, -1, width) for g in (user_first_g, user_second_g, item_first_g, item_second_g)],
        axis=1,
    )
    terms, rest = [], loss_part
    for _ in range(3):
        terms.append(lax.reduce_precision(rest, 8, 7))
        rest = rest - terms[-1]
    loss_row = jnp.concatenate([jnp.stack(terms), jnp.zeros(width - 3, jnp.float32)])
    sent = exchange(
        jnp.concatenate(
            [
                slot_grads.reshape(n_all, cap, width),
                weight_g,
                jnp.broadcast_to(loss_row, (n_all, 1, width)),
            ],
            axis=1,
        ).astype(jnp.bfloat16)
    )
    chunk = jnp.sum(sent[:, cap:-1].astype(jnp.float32), axis=0) / n_all
    whole = exchange(jnp.broadcast_to(chunk.astype(jnp.bfloat16)[None], weight_g.shape))
    mean_loss = jnp.sum(sent[:, -1, :3].astype(jnp.float32)) / (n_all * n_ex)

    grad_rows = (
        jnp.zeros_like(id_table)
        .at[asked.reshape(-1)]
        .add(sent[:, :cap].astype(jnp.float32).reshape(-1, width), mode="promise_in_bounds")
    )
    new_state = ada_state + jnp.mean(grad_rows * grad_rows, axis=1)
    new_table = id_table - learn_rate * grad_rows / (jnp.sqrt(new_state)[:, None] + epsilon)
    outs = []
    at = 0
    for w in (user_first, user_second, item_first, item_second):
        rows = w.size // (n_all * width)
        outs.append(whole[:, at : at + rows].astype(jnp.float32).reshape(w.shape))
        at += rows
    return (new_table, new_state, *outs, mean_loss)


def solution(mesh):
    return jax.shard_map(
        per_device,
        mesh=mesh,
        in_specs=(
            P(("dp", "shard"), None),
            P(("dp", "shard")),
            P(),
            P(),
            P(),
            P(),
            P(("dp", "shard"), None, None, None),
            P(("dp", "shard"), None),
        ),
        out_specs=(P(("dp", "shard"), None), P(("dp", "shard")), P(), P(), P(), P(), P()),
        check_vma=False,
    )
```

time: 363 us -> 195 us (0.54)
  waiting for transfers between devices: 135 us -> 35.8 us
  blocking collectives: 99.8 us -> 48.2 us
  between operations: 16.3 us -> 7.1 us
  matrix products: 41 us -> 33.2 us
  other arithmetic: 45.6 us -> 40.9 us
    psum x1 -> x0, waiting for transfers between devices: 96.8 us -> none  [per_device(): lax.psum((user_first_g, user_second_g, item_first_g, item_second_g, loss_...]
    psum x1 -> x0, blocking collectives: 40.8 us -> none  [per_device(): lax.psum((user_first_g, user_second_g, item_first_g, item_second_g, loss_...]
    all_gather x2 -> x0, blocking collectives: 20.4 us -> none  [the longest x1 11.5 us: per_device(): lax.all_gather(user_vec, 'dp', axis=0, tiled=True).astype(jnp.bfloat16)]
    all_to_all x3 -> x2, blocking collectives: 38.6 us -> 48.2 us  [exchange(): return lax.all_to_all(x, AXES, split_axis=0, concat_axis=0, tiled=True)]
    ppermute x0 -> x9, starting transfers between devices: none -> 8.74 us  [the longest x6 5.61 us: from_peers(): lax.ppermute(blocks[k], 'dp', [(i, (i + k) % n) for i in range(n)])]
    all_gather x1 -> x0, waiting for transfers between devices: 8.37 us -> none  [per_device(): lax.all_gather(item_bf, 'dp', axis=0, tiled=True)]
    all_to_all x3 -> x2, starting transfers between devices: 11.6 us -> 5.39 us  [exchange(): return lax.all_to_all(x, AXES, split_axis=0, concat_axis=0, tiled=True)]
    ppermute x0 -> x9, waiting for transfers between devices: none -> 5.62 us  [the longest x6 5.61 us: from_peers(): lax.ppermute(blocks[k], 'dp', [(i, (i + k) % n) for i in range(n)])]
  transfers between devices with their start and end apart: 5 -> 11, of which waited for: 4 -> 2; matrix products, arithmetic and copies ran while one was open for 4% -> 24% of each run, Pallas kernels for 0% -> 0%
where the time goes in v1:
time: 195 us
  blocking collectives  48.2 us (25%)
  other arithmetic  40.9 us (21%)
  waiting for transfers between devices  35.8 us (18%)
  matrix products  33.2 us (17%)
  local copies, waits for them, and re-layouts  15.2 us (8%)
  starting transfers between devices  14.1 us (7%)
  between operations  7.1 us (4%)
    all_to_all x2, blocking collectives, exchange(): return lax.all_to_all(x, AXES, split_axis=0, concat_axis=0, tiled=True)  48.2 us
    all_to_all x2, waiting for transfers between devices, exchange(): return lax.all_to_all(x, AXES, split_axis=0, concat_axis=0, tiled=True)  30.2 us
    scatter-add x1, other arithmetic, per_device(): grad_rows = jnp.zeros_like(id_table).at[asked.reshape(-1)].add(sent[:, :c...  15.7 us
    dot_general x6, matrix products, tower_pass(): jnp.dot(hidden_act, second_w, precision=highest, preferred_element_type=j...  15.1 us
    scatter-add x1, other arithmetic, per_device(): jnp.zeros_like(slot_rows).at[slot_index]  9.61 us
    dot_general x6, matrix products, tower_pass(): jnp.dot(looked, first_w, precision=highest, preferred_element_type=jnp.fl...  9.15 us
    gather x1, local copies, waits for them, and re-layouts, per_device(): fetched = id_table.at[asked.reshape(-1)].get(mode='promise_in_bounds')  7.28 us
    ppermute x6, waiting for transfers between devices, from_peers(): lax.ppermute(blocks[k], 'dp', [(i, (i + k) % n) for i in range(n)])  5.61 us
  transfers between devices with their start and end apart: 11, of which 2 were waited for; matrix products, arithmetic and copies ran while one was open for 24% of the time, Pallas kernels for 0%

profile of v1, /device:TPU:0, one launch (start us, length us, event | category | flops | bytes accessed | tf_op | source)
XLA Modules:
  0.0 194.6 jit_solution(5036669770508211283)
XLA Ops:
  0.6 14.4 %all_to_all.24 = s32[32,1,72]{2,1,0:T(1,128)S(1)} all-to-all(s32[32,1,72]{2,1,0:T(1,128)} %bitcast.72), channel_id=1, replica_groups=mesh['dp'=4,'shard'=8] {'dp','shard'}, dimensions={0} | all-to-all | bytes 18432 | tf_op jit(solution)/shard_map/all_to_all | solution.py:24
  16.4 7.3 %gather_fusion = f32[2304,128]{1,0:T(8,128)} fusion(f32[8192,128]{1,0:T(8,128)} %param.8, s32[3072]{0:T(1024)S(1)} %pad_clamp_fusion), kind=kCustom, calls=%fused_computation | custom fusion | bytes 2368512 | tf_op jit(solution)/shard_map/gather | solution.py:50
  23.7 2.8 %all-to-all-start.1 = ((f32[32,72,128]{2,1,0:T(8,128)}), f32[32,72,128]{2,1,0:T(8,128)S(1)}, u32[]{:S(2)}, u32[]{:S(2)}) async-start(f32[32,72,128]{2,1,0:T(8,128)} %bitcast.2), calls=%async_computation.1 | async-start | bytes 2359296 | tf_op jit(solution)/shard_map/all_to_all | solution.py:24
  26.6 30.2 %all-to-all-done.1 = f32[32,72,128]{2,1,0:T(8,128)S(1)} async-done(((f32[32,72,128]{2,1,0:T(8,128)}), f32[32,72,128]{2,1,0:T(8,128)S(1)}, u32[]{:S(2)}, u32[]{:S(2)}) %all-to-all-start.1) | async-done | bytes 1179680 | tf_op jit(solution)/shard_map/all_to_all | solution.py:24
  56.8 2.6 %gather_fusion.1 = f32[1536,128]{1,0:T(8,128)S(1)} fusion(f32[2304,128]{1,0:T(8,128)S(1)} %bitcast.63, s32[2048]{0:T(1024)S(1)} %pad_clamp_fusion.1), kind=kCustom, calls=%fused_computation.1 | custom fusion | bytes 1579008 | tf_op jit(solution)/shard_map/gather | solution.py:53
  60.4 1.5 multiply_reduce_fusion.4
  62.6 1.8 fusion.23
  64.4 2.7 %multiply_reduce_fusion.2 = (f32[1024]{0:T(1024)S(1)}, f32[1024,128]{0,1:T(8,128)S(1)}) fusion(f32[512,128]{1,0:T(8,128)S(1)} %copy-done, f32[1024,512]{1,0:T(8,128)S(1)} %fusion.23), kind=kOutput, calls=%fused_computation.54 | convolution fusion | flops 807664640 | bytes 2887680 | tf_op jit(solution)/shard_map/jvp()/dot_general | solution.py:19
  68.5 1.5 collective-permute-start
  70.5 5.6 %collective-permute-done = bf16[512,128]{0,1:T(8,128)(2,1)S(1)} collective-permute-done((bf16[512,128]{0,1:T(8,128)(2,1)S(1)}, bf16[512,128]{0,1:T(8,128)(2,1)S(1)}, u32[]{:S(2)}, u32[]{:S(2)}) %collective-permute-start) | collective-permute-done | bytes 131104 | tf_op jit(solution)/shard_map/ppermute | solution.py:30
  81.9 1.9 collective-permute-start.1
  90.0 4.3 %convolution_convert_fusion = bf16[512,128]{1,0:T(8,128)(2,1)} fusion(f32[1024,512]{1,0:T(8,128)S(1)} %fusion.23, f32[1024,128]{0,1:T(8,128)S(1)} %get-tuple-element.38, f32[512,128]{0,1:T(8,128)S(1)} %get-tuple-element.20, f32[512,128]{0,1:T(8,128)S(1)} %get-tuple-element.19, f32[1024]{0:T(1024)S(1)} %multiply_multiply_fusion, f32[1024]{0:T(1024)S(1)} %get-tuple-element.34), kind=kOutput, calls=%fused_computation.26 | convolution fusion | flops 808255488 | bytes 3284992 | tf_op jit(solution)/shard_map/transpose(jvp())/dot_general | solution.py:19
  94.4 2.5 %fusion.1 = f32[1024,512]{1,0:T(8,128)S(1)} fusion(f32[1024,512]{1,0:T(8,128)S(1)} %fusion.23, f32[512,128]{1,0:T(8,128)S(1)} %copy-done, f32[1024,128]{0,1:T(8,128)S(1)} %get-tuple-element.38, f32[512,128]{0,1:T(8,128)S(1)} %get-tuple-element.20, f32[512,128]{0,1:T(8,128)S(1)} %get-tuple-element.19, f32[1024]{0:T(1024)S(1)} %multiply_multiply_fusion, ...), kind=kOutput, calls=%fused_computation.8 | convolution fusion | flops 810811392 | bytes 5513216 | tf_op jit(solution)/shard_map/transpose(jvp())/dot_general | solution.py:19
  96.8 2.6 %fusion.51 = f32[1024,128]{1,0:T(8,128)} fusion(f32[1024,512]{1,0:T(8,128)S(1)} %fusion.1, f32[128,512]{1,0:T(8,128)S(1)} %copy-done.9), kind=kOutput, calls=%fused_computation.118 | convolution fusion | flops 805306368 | bytes 2883584 | tf_op jit(solution)/shard_map/transpose(jvp())/dot_general | solution.py:17
  99.4 2.0 %convolution_convert_fusion.1 = bf16[128,512]{1,0:T(8,128)(2,1)} fusion(f32[1024,512]{1,0:T(8,128)S(1)} %fusion.1, f32[1536,128]{1,0:T(8,128)S(1)} %gather_fusion.1), kind=kOutput, calls=%fused_computation.27 | convolution fusion | flops 805371904 | bytes 2752512 | tf_op jit(solution)/shard_map/transpose(jvp())/dot_general | solution.py:17
  106.6 2.6 %maximum_convert_fusion = bf16[128]{0:T(256)(128)(2,1)} fusion(bf16[125]{0:T(256)(128)(2,1)S(1)} %broadcast_in_dim.48, bf16[1]{0:T(256)(128)(2,1)} %bitcast.25, f32[1]{0:T(128)} %bitcast.24, f32[1]{0:T(128)} %bitcast.23), kind=kLoop, calls=%fused_computation.104 | loop fusion | flops 1024 | bytes 516 | tf_op jit(solution)/shard_map/convert.16
  109.2 1.7 multiply_reduce_fusion.3
  111.6 2.8 %convolution_convert_fusion.2 = bf16[512,128]{1,0:T(8,128)(2,1)} fusion(f32[512,512]{1,0:T(8,128)S(1)} %copy-done.4, f32[512,128]{0,1:T(8,128)S(1)} %copy-done.8, f32[512,128]{0,1:T(8,128)S(1)} %get-tuple-element.14, f32[512]{0:T(512)S(1)} %multiply_multiply_fusion.1, f32[512]{0:T(512)S(1)} %get-tuple-element.36), kind=kOutput, calls=%fused_computation.28 | convolution fusion | flops 404094976 | bytes 1708032 | tf_op jit(solution)/shard_map/transpose(jvp())/dot_general | solution.py:19
  117.6 9.6 %scatter_custom_fusion = f32[2304,128]{1,0:T(8,128)S(1)} fusion(s32[1536]{0:T(1024)} %copy-done.12, f32[1024,128]{1,0:T(8,128)S(1)} %copy-done.2, f32[]{:T(128)} %constant.62, f32[512,128]{1,0:T(8,128)S(1)} %fusion.50, f32[]{:T(128)} %constant.13.clone.1), kind=kCustom, calls=%fused_computation.45 | custom fusion | flops 393216 | bytes 1967104 | tf_op jit(solution)/shard_map/scatter-add | solution.py:97
  128.3 33.8 %all_to_all.25 = bf16[32,137,128]{2,1,0:T(8,128)(2,1)S(1)} all-to-all(bf16[32,137,128]{2,1,0:T(8,128)(2,1)S(1)} %constant_dynamic-update-slice_fusion), channel_id=1, replica_groups=mesh['dp'=4,'shard'=8] {'dp','shard'}, dimensions={0} | all-to-all | bytes 2244608 | tf_op jit(solution)/shard_map/all_to_all | solution.py:24
  163.0 2.6 %all-to-all-start.3 = ((bf16[32,64,128]{2,1,0:T(8,128)(2,1)}), bf16[32,64,128]{2,1,0:T(8,128)(2,1)S(1)}, u32[]{:S(2)}, u32[]{:S(2)}) async-start(bf16[32,64,128]{2,1,0:T(8,128)(2,1)} %broadcast_in_dim.50), calls=%async_computation.3 | async-start | bytes 1048576 | tf_op jit(solution)/shard_map/all_to_all | solution.py:24
  165.7 15.7 %scatter_custom_fusion.1 = f32[8192,128]{1,0:T(8,128)} fusion(s32[2304]{0:T(1024)S(1)} %fusion.36, f32[]{:T(128)} %constant.13.clone.1, bf16[2304,128]{1,0:T(8,128)(2,1)S(1)} %bitcast.64), kind=kCustom, calls=%fused_computation.19 | custom fusion | flops 589824 | bytes 4784132 | tf_op jit(solution)/shard_map/scatter-add | solution.py:124
  181.4 3.5 %multiply_reduce_fusion = f32[8192]{0:T(1024)S(1)} fusion(f32[8192,128]{1,0:T(8,128)} %scatter_custom_fusion.1), kind=kLoop, calls=%fused_computation.5 | loop fusion | flops 2088960 | bytes 4227072 | tf_op jit(solution)/shard_map/reduce_sum | solution.py:126
  185.5 4.2 %divide_subtract_fusion = f32[8192,128]{1,0:T(8,128)} fusion(f32[8192,128]{1,0:T(8,128)S(1)} %copy-done.1, f32[8192,128]{1,0:T(8,128)} %scatter_custom_fusion.1, f32[8192]{0:T(1024)S(1)} %get-tuple-element.7), kind=kLoop, calls=%fused_computation.4 | loop fusion | flops 3145728 | bytes 12615680 | tf_op jit(solution)/shard_map/sub | solution.py:127
  (114 shorter events, 27.3 us)
Async XLA Ops:
  0.6 63.8 %copy-start = (f32[512,128]{1,0:T(8,128)S(1)}, f32[512,128]{1,0:T(8,128)}, u32[]{:S(2)}) copy-start(f32[512,128]{1,0:T(8,128)} %param.13) | copy-start | bytes 786436
  23.7 2.8 %copy-start.16 = (s32[1,1536]{1,0:T(1,128)S(1)}, s32[1,1536]{1,0:T(1,128)}, u32[]{:S(2)}) copy-start(s32[1,1536]{1,0:T(1,128)} %param.15) | copy-start | bytes 18436
  23.7 33.1 %all-to-all-start.1 = ((f32[32,72,128]{2,1,0:T(8,128)}), f32[32,72,128]{2,1,0:T(8,128)S(1)}, u32[]{:S(2)}, u32[]{:S(2)}) async-start(f32[32,72,128]{2,1,0:T(8,128)} %bitcast.2), calls=%async_computation.1 | async-start | bytes 2359296 | tf_op jit(solution)/shard_map/all_to_all | solution.py:24
  26.6 30.2 %copy-start.12 = (s32[1536]{0:T(1024)}, s32[1536]{0:T(1024)S(1)}, u32[]{:S(2)}) copy-start(s32[1536]{0:T(1024)S(1)} %fusion.37) | copy-start | bytes 18436
  56.8 2.6 %copy-start.5 = (f32[128,512]{1,0:T(8,128)S(1)}, f32[128,512]{1,0:T(8,128)}, u32[]{:S(2)}) copy-start(f32[128,512]{1,0:T(8,128)} %param.10) | copy-start | bytes 786436
  56.8 3.6 %copy-start.18 = (f32[512,128]{1,0:T(8,128)S(1)}, f32[512,128]{1,0:T(8,128)}, u32[]{:S(2)}) copy-start(f32[512,128]{1,0:T(8,128)} %param.11) | copy-start | bytes 786436
  60.4 2.2 %copy-start.9 = (f32[128,512]{1,0:T(8,128)S(1)}, f32[128,512]{1,0:T(8,128)}, u32[]{:S(2)}) copy-start(f32[128,512]{1,0:T(8,128)} %param.12) | copy-start | bytes 786436
  61.9 5.3 %copy-start.14 = (f32[512]{0:T(512)}, f32[512]{0:T(512)S(1)}, u32[]{:S(2)}) copy-start(f32[512]{0:T(512)S(1)} %get-tuple-element.39) | copy-start | bytes 6148
  61.9 5.3 %copy-start.7 = (f32[512,128]{0,1:T(8,128)}, f32[512,128]{0,1:T(8,128)S(1)}, u32[]{:S(2)}) copy-start(f32[512,128]{0,1:T(8,128)S(1)} %get-tuple-element.40) | copy-start | bytes 786436
  67.3 9.9 %collective-permute-start.4 = (bf16[512,128]{0,1:T(8,128)(2,1)S(1)}, bf16[512,128]{0,1:T(8,128)(2,1)S(1)}, u32[]{:S(2)}, u32[]{:S(2)}) collective-permute-start(bf16[512,128]{0,1:T(8,128)(2,1)S(1)} %get-tuple-element.12), channel_id=1, source_target_pairs={{0,24},{8,0},{16,8},{24,16},{1,25},{9,1},{17,9},{25,17},{2,26},{10... | collective-permute-start | bytes 393224 | tf_op jit(solution)/shard_map/ppermute | solution.py:30
  67.9 8.7 %collective-permute-start.2 = (bf16[512,128]{0,1:T(8,128)(2,1)S(1)}, bf16[512,128]{0,1:T(8,128)(2,1)S(1)}, u32[]{:S(2)}, u32[]{:S(2)}) collective-permute-start(bf16[512,128]{0,1:T(8,128)(2,1)S(1)} %get-tuple-element.12), channel_id=1, source_target_pairs={{0,16},{8,24},{16,0},{24,8},{1,17},{9,25},{17,1},{25,9},{2,18},{10... | collective-permute-start | bytes 393224 | tf_op jit(solution)/shard_map/ppermute | solution.py:30
  68.5 7.6 %collective-permute-start = (bf16[512,128]{0,1:T(8,128)(2,1)S(1)}, bf16[512,128]{0,1:T(8,128)(2,1)S(1)}, u32[]{:S(2)}, u32[]{:S(2)}) collective-permute-start(bf16[512,128]{0,1:T(8,128)(2,1)S(1)} %get-tuple-element.12), channel_id=1, source_target_pairs={{0,8},{8,16},{16,24},{24,0},{1,9},{9,17},{17,25},{25,1},{2,10},{10... | collective-permute-start | bytes 393224 | tf_op jit(solution)/shard_map/ppermute | solution.py:30
  77.8 9.5 %collective-permute-start.8 = (f32[4,512]{1,0:T(4,128)S(1)}, f32[4,512]{1,0:T(4,128)S(1)}, u32[]{:S(2)}, u32[]{:S(2)}) collective-permute-start(f32[4,512]{1,0:T(4,128)S(1)} %pad_maximum_fusion.1), channel_id=1, source_target_pairs={{0,24},{8,0},{16,8},{24,16},{1,25},{9,1},{17,9},{25,17},{2,26},{10... | collective-permute-start | bytes 24584 | tf_op jit(solution)/shard_map/ppermute | solution.py:30
  78.9 8.5 %collective-permute-start.7 = (f32[4,512]{1,0:T(4,128)S(1)}, f32[4,512]{1,0:T(4,128)S(1)}, u32[]{:S(2)}, u32[]{:S(2)}) collective-permute-start(f32[4,512]{1,0:T(4,128)S(1)} %pad_maximum_fusion.1), channel_id=1, source_target_pairs={{0,16},{8,24},{16,0},{24,8},{1,17},{9,25},{17,1},{25,9},{2,18},{10... | collective-permute-start | bytes 24584 | tf_op jit(solution)/shard_map/ppermute | solution.py:30
  79.8 7.6 %collective-permute-start.6 = (f32[4,512]{1,0:T(4,128)S(1)}, f32[4,512]{1,0:T(4,128)S(1)}, u32[]{:S(2)}, u32[]{:S(2)}) collective-permute-start(f32[4,512]{1,0:T(4,128)S(1)} %pad_maximum_fusion.1), channel_id=1, source_target_pairs={{0,8},{8,16},{16,24},{24,0},{1,9},{9,17},{17,25},{25,1},{2,10},{10... | collective-permute-start | bytes 24584 | tf_op jit(solution)/shard_map/ppermute | solution.py:30
  81.9 27.3 %collective-permute-start.1 = (bf16[512,128]{0,1:T(8,128)(2,1)}, bf16[512,128]{0,1:T(8,128)(2,1)}, u32[]{:S(2)}, u32[]{:S(2)}) collective-permute-start(bf16[512,128]{0,1:T(8,128)(2,1)} %convolution_convert_fusion.6), channel_id=1, source_target_pairs={{0,24},{8,0},{16,8},{24,16},{1,25},{9,1},{17,9},{25,17},{2,26},{10... | collective-permute-start | bytes 393224 | tf_op jit(solution)/shard_map/ppermute | solution.py:37
  85.0 24.2 %collective-permute-start.3 = (bf16[512,128]{0,1:T(8,128)(2,1)}, bf16[512,128]{0,1:T(8,128)(2,1)}, u32[]{:S(2)}, u32[]{:S(2)}) collective-permute-start(bf16[512,128]{0,1:T(8,128)(2,1)} %convolution_convert_fusion.5), channel_id=1, source_target_pairs={{0,16},{8,24},{16,0},{24,8},{1,17},{9,25},{17,1},{25,9},{2,18},{10... | collective-permute-start | bytes 393224 | tf_op jit(solution)/shard_map/ppermute | solution.py:37
  87.3 22.0 %collective-permute-start.5 = (bf16[512,128]{0,1:T(8,128)(2,1)}, bf16[512,128]{0,1:T(8,128)(2,1)}, u32[]{:S(2)}, u32[]{:S(2)}) collective-permute-start(bf16[512,128]{0,1:T(8,128)(2,1)} %convolution_convert_fusion.4), channel_id=1, source_target_pairs={{0,8},{8,16},{16,24},{24,0},{1,9},{9,17},{17,25},{25,1},{2,10},{10... | collective-permute-start | bytes 393224 | tf_op jit(solution)/shard_map/ppermute | solution.py:37
  106.6 5.0 %copy-start.4 = (f32[512,512]{1,0:T(8,128)S(1)}, f32[512,512]{1,0:T(8,128)}, u32[]{:S(2)}) copy-start(f32[512,512]{1,0:T(8,128)} %copy-done.3) | copy-start | bytes 3145732
  106.6 5.0 %copy-start.8 = (f32[512,128]{0,1:T(8,128)S(1)}, f32[512,128]{0,1:T(8,128)}, u32[]{:S(2)}) copy-start(f32[512,128]{0,1:T(8,128)} %copy-done.7) | copy-start | bytes 786436
  111.6 2.8 %copy-start.19 = (f32[512,128]{1,0:T(8,128)S(1)}, f32[512,128]{1,0:T(8,128)}, u32[]{:S(2)}) copy-start(f32[512,128]{1,0:T(8,128)} %param.11) | copy-start | bytes 786436
  163.0 28.0 %all-to-all-start.3 = ((bf16[32,64,128]{2,1,0:T(8,128)(2,1)}), bf16[32,64,128]{2,1,0:T(8,128)(2,1)S(1)}, u32[]{:S(2)}, u32[]{:S(2)}) async-start(bf16[32,64,128]{2,1,0:T(8,128)(2,1)} %broadcast_in_dim.50), calls=%async_computation.3 | async-start | bytes 1048576 | tf_op jit(solution)/shard_map/all_to_all | solution.py:24
  181.4 3.5 %copy-start.13 = (f32[8192]{0:T(1024)S(1)}, f32[8192]{0:T(1024)}, u32[]{:S(2)}) copy-start(f32[8192]{0:T(1024)} %param.9) | copy-start | bytes 98308
  181.4 4.1 %copy-start.1 = (f32[8192,128]{1,0:T(8,128)S(1)}, f32[8192,128]{1,0:T(8,128)}, u32[]{:S(2)}) copy-start(f32[8192,128]{1,0:T(8,128)} %param.8) | copy-start | bytes 12582916
  (7 other events, 8.9 us)

commit v2 on v1

v2 whole, which is shorter than its diff:
```python
import functools

import jax
import jax.numpy as jnp
from jax import lax
from jax.experimental import pallas as pl
from jax.experimental.pallas import tpu as pltpu
from jax.sharding import PartitionSpec as P

EXAMPLES_ON_CHIP = 512
AXES = ("dp", "shard")

fine = lax.Precision.HIGH
logit_divisor = 0.025
learn_rate = 0.1
epsilon = 1e-08


def product(a, b, dims):
    return lax.dot_general(
        a, b, (dims, ((), ())), precision=fine, preferred_element_type=jnp.float32
    )


def tower(looked, first_w, second_w):
    hidden = product(looked, first_w, ((1,), (0,)))
    gate = jax.nn.sigmoid(hidden)
    active = hidden * gate
    out = product(active, second_w, ((1,), (0,)))
    norm = jnp.sqrt(jnp.sum(out * out, axis=1, keepdims=True) + 1e-06)
    return out / norm, (looked, hidden, out, first_w, second_w)


def halves(x):
    high = x.astype(jnp.bfloat16)
    return high, (x - high.astype(jnp.float32)).astype(jnp.bfloat16)


def wide_dot(a, b, dims):
    def one(p, q):
        return lax.dot_general(p, q, (dims, ((), ())), preferred_element_type=jnp.float32)

    (ah, al), (bh, bl) = a, b
    return one(ah, bh) + one(al, bh) + one(ah, bl)


def back_kernel(last, *refs):
    looked, hidden, out, cot, first_w, second_w = refs[:6]
    first_g, second_g = refs[-2:]
    look_g = refs[-3] if last else refs[6]
    step = pl.program_id(0)

    @pl.when(step == 0)
    def _():
        first_g[...] = jnp.zeros_like(first_g)
        second_g[...] = jnp.zeros_like(second_g)

    z, g, h = out[...], cot[...], hidden[...]
    rows, width = z.shape
    inverse = 1.0 / jnp.sqrt(jnp.sum(z * z, axis=1, keepdims=True) + 1e-06)
    vec = z * inverse
    out_cot = (g - vec * jnp.sum(vec * g, axis=1, keepdims=True)) * inverse
    gate = 1.0 / (1.0 + jnp.exp(-h))
    active = h * gate
    slope = gate + active * (1.0 - gate)
    hidden_cot = wide_dot(halves(out_cot), halves(second_w[...]), ((1,), (1,))) * slope
    both = halves(hidden_cot)
    mine = wide_dot(both, halves(first_w[...]), ((1,), (1,))).astype(look_g.dtype)
    if last:
        look_g[pl.ds(pl.multiple_of(step * rows, rows), rows), :] = mine
    else:
        look_g[...] = mine
    first_g[...] += wide_dot(halves(looked[...].T), both, ((1,), (0,)))
    second_g[...] += wide_dot(halves(out_cot.T), halves(active), ((1,), (0,)))

    @pl.when(step == pl.num_programs(0) - 1)
    def _():
        flat = [first_g[:, c : c + width] for c in range(0, first_g.shape[1], width)]
        flat += [second_g[:, c : c + width].T for c in range(0, second_g.shape[1], width)]
        flat = [f.astype(jnp.bfloat16) for f in flat]
        if not last:
            for k, f in enumerate(flat):
                refs[7][k * width : (k + 1) * width, :] = f
            return
        item_look, item_sums, lookups, loss_row, sent = refs[6:11]
        n_all = sent.shape[0]
        deep = 2 * len(flat) * width // n_all
        cap = sent.shape[1] - deep - 8
        for k in range(n_all):
            block, at = divmod(k * deep, width)
            if block < len(flat):
                piece = flat[block][at : at + deep]
            else:
                at += (block - len(flat)) * width
                piece = item_sums[at : at + deep, :]
            sent[k, :deep, :] = piece
            sent[k, deep : deep + 8, :] = jnp.broadcast_to(loss_row[...], (8, width)).astype(
                sent.dtype
            )
        n_ex = look_g.shape[0]
        group = max(1, 576 // cap)
        user_ids, item_ids = lookups[:, :n_ex], lookups[:, n_ex:]
        for k in range(0, n_all, group):
            n = min(group, n_all - k)

            def owns(ids):
                slot = lax.broadcasted_iota(jnp.int32, (n * cap, ids.shape[1]), 0) + k * cap
                return jnp.where(slot == ids, 1.0, 0.0).astype(jnp.bfloat16)

            total = jnp.dot(owns(user_ids), look_g[...], preferred_element_type=jnp.float32)
            total += jnp.dot(owns(item_ids), item_look[...], preferred_element_type=jnp.float32)
            for j in range(n):
                sent[k + j, deep + 8 :, :] = total[j * cap : (j + 1) * cap].astype(sent.dtype)


def tower_back(saved, cot, rest=(), n_all=0, cap=0):
    looked, hidden, out, first_w, second_w = saved
    n, width = looked.shape
    inner = hidden.shape[1]
    rows = min(n, 256)
    last = bool(rest)

    def by_rows(w):
        return pl.BlockSpec((rows, w), lambda i: (i, 0))

    def fixed(shape):
        return pl.BlockSpec(shape, lambda i: (0,) * len(shape))

    if last:
        shape = (n_all, 4 * inner // n_all + 8 + cap, width)
        out_specs = fixed(shape)
        out_shape = jax.ShapeDtypeStruct(shape, jnp.bfloat16)
        scratch = [pltpu.VMEM((n, width), jnp.bfloat16)]
    else:
        out_specs = [by_rows(width), fixed((2 * inner, width))]
        out_shape = [
            jax.ShapeDtypeStruct((n, width), jnp.bfloat16),
            jax.ShapeDtypeStruct((2 * inner, width), jnp.bfloat16),
        ]
        scratch = []
    return pl.pallas_call(
        functools.partial(back_kernel, last),
        grid=(n // rows,),
        in_specs=[by_rows(width), by_rows(inner), by_rows(width), by_rows(width)]
        + [fixed(x.shape) for x in (first_w, second_w, *rest)],
        out_specs=out_specs,
        out_shape=out_shape,
        scratch_shapes=scratch + [pltpu.VMEM((width, inner), jnp.float32)] * 2,
        cost_estimate=pl.CostEstimate(
            flops=24 * n * width * inner,
            transcendentals=n * inner,
            bytes_accessed=4 * n * (inner + 4 * width),
        ),
        name="user_back" if last else "item_back",
    )(looked, hidden, out, cot, first_w, second_w, *rest)


def update_kernel(skip, rows_ref, grads, table, state, new_table, new_state, *totals):
    step = pl.program_id(0)

    @pl.when(step == 0)
    def _():
        for total in totals:
            total[...] = jnp.zeros_like(total)
        n_from, _, cap = rows_ref.shape
        each = n_from // len(totals)

        def body(i, carry):
            come = [grads[q * each + i, skip:, :].astype(jnp.float32) for q in range(len(totals))]
            for c in range(cap):
                for q, total in enumerate(totals):
                    row = rows_ref[q * each + i, 0, c]
                    total[pl.ds(row, 1), :] += come[q][c : c + 1, :]
            return carry

        lax.fori_loop(0, each, body, 0)

    rows, width = table.shape
    for k in range(rows // width):
        here = pl.ds(pl.multiple_of(step * rows + k * width, width), width)
        g = totals[0][here, :]
        for total in totals[1:]:
            g = g + total[here, :]
        mean = jnp.sum((g * g).T, axis=0, keepdims=True) * (1.0 / width)
        now = state[k : k + 1, :] + mean
        new_state[k : k + 1, :] = now
        scale = learn_rate / (jnp.sqrt(now) + epsilon)
        scale = jnp.broadcast_to(scale, (width, width)).T
        block = slice(k * width, (k + 1) * width)
        new_table[block, :] = table[block, :] - g * scale


def update(table, state, rows_of, grads):
    n, width = table.shape
    rows = n // 2
    lanes = 4
    state = state.reshape(-1, width)
    skip = grads.shape[1] - rows_of.shape[2]
    new_table, new_state = pl.pallas_call(
        functools.partial(update_kernel, skip),
        grid_spec=pltpu.PrefetchScalarGridSpec(
            num_scalar_prefetch=1,
            grid=(n // rows,),
            in_specs=[
                pl.BlockSpec(grads.shape, lambda i, r: (0, 0, 0)),
                pl.BlockSpec((rows, width), lambda i, r: (i, 0)),
                pl.BlockSpec((rows // width, width), lambda i, r: (i, 0)),
            ],
            out_specs=[
                pl.BlockSpec((rows, width), lambda i, r: (i, 0)),
                pl.BlockSpec((rows // width, width), lambda i, r: (i, 0)),
            ],
            scratch_shapes=[pltpu.VMEM(table.shape, jnp.float32)] * lanes,
        ),
        out_shape=[
            jax.ShapeDtypeStruct(table.shape, jnp.float32),
            jax.ShapeDtypeStruct(state.shape, jnp.float32),
        ],
        cost_estimate=pl.CostEstimate(
            flops=20 * n * width, transcendentals=n, bytes_accessed=8 * n * width
        ),
        name="update",
    )(rows_of, grads, table, state)
    return new_table, new_state.reshape(-1)


def spread_kernel(place, *refs):
    n_dp = len(refs) - 5
    pieces, outs, whole = refs[:n_dp], refs[n_dp:-1], refs[-1]
    n_sh, rows, width = pieces[0].shape
    for k, piece in enumerate(pieces):
        for j in range(n_sh):
            d = lax.rem(place[0] + k, n_dp)
            s = lax.rem(place[1] + j, n_sh)
            at = pl.multiple_of((d * n_sh + s) * rows, rows)
            whole[pl.ds(at, rows), :] = piece[j].astype(jnp.float32)
    at = 0
    for first, second in (outs[:2], outs[2:]):
        for c in range(0, first.shape[1], width):
            first[:, c : c + width] = whole[at : at + width, :]
            at += width
        second[...] = whole[at : at + second.shape[0], :]
        at += second.shape[0]


def spread(pieces, weights):
    place = jnp.stack([lax.axis_index("dp"), lax.axis_index("shard")]).astype(jnp.int32)
    total = sum(w.size for w in weights)
    return pl.pallas_call(
        spread_kernel,
        in_specs=[pl.BlockSpec(memory_space=pltpu.SMEM)]
        + [pl.BlockSpec(memory_space=pltpu.VMEM)] * len(pieces),
        out_specs=[pl.BlockSpec(memory_space=pltpu.VMEM)] * 4,
        out_shape=[jax.ShapeDtypeStruct(w.shape, jnp.float32) for w in weights],
        scratch_shapes=[
            pltpu.VMEM((total // pieces[0].shape[-1], pieces[0].shape[-1]), jnp.float32)
        ],
        cost_estimate=pl.CostEstimate(flops=total, transcendentals=0, bytes_accessed=6 * total),
        name="spread",
    )(place, *pieces)


def middle_kernel(n_dp, n_ex, *refs):
    expos, seen, users = refs[:n_dp], refs[n_dp : 2 * n_dp], refs[2 * n_dp : 3 * n_dp]
    own, positive, item_cot, share, loss_row = refs[3 * n_dp :]
    step = pl.program_id(0)
    totals = []
    for b in range(n_dp):
        total = seen[0][b : b + 1, :]
        for k in range(1, n_dp):
            j = (b - k) % n_dp
            total = total + seen[k][j : j + 1, :]
        totals.append(total)
    acc = jnp.zeros(item_cot.shape, jnp.float32)
    for expo, total, user in zip(expos, totals, users):
        probs = (expo[...] * (1.0 / total)).astype(jnp.bfloat16)
        acc = acc + jnp.dot(probs, user[...], preferred_element_type=jnp.float32)
    rows = item_cot.shape[0]
    own_f = own[...].astype(jnp.float32)
    acc = acc - jnp.where(step * rows < n_ex, own_f, jnp.zeros_like(own_f))
    item_cot[...] = acc / logit_divisor

    @pl.when(step == 0)
    def _():
        width = share.shape[1]
        share[...] = jnp.broadcast_to(1.0 / totals[0], (width, n_ex)).T
        pairs = users[0][...].astype(jnp.float32) * positive[...].astype(jnp.float32)
        score = jnp.sum(jnp.sum(pairs, axis=0, keepdims=True), axis=1, keepdims=True)
        loss = jnp.sum(jnp.log(totals[0]), axis=1, keepdims=True) - score / logit_divisor
        rest = jnp.broadcast_to(loss, loss_row.shape)
        lane = lax.broadcasted_iota(jnp.int32, loss_row.shape, 1)
        row = jnp.zeros(loss_row.shape, jnp.float32)
        for k in range(3):
            term = rest.astype(jnp.bfloat16).astype(jnp.float32)
            row = jnp.where(lane == k, term, row)
            rest = rest - term
        loss_row[...] = row


def middle(expos, seen, users, items):
    n_dp = len(expos)
    n_items, n_ex = expos[0].shape
    width = items.shape[1]
    rows = 256
    last = n_ex // rows - 1

    def fixed(x):
        return pl.BlockSpec(x.shape, lambda i: (0, 0))

    return pl.pallas_call(
        functools.partial(middle_kernel, n_dp, n_ex),
        grid=(n_items // rows,),
        in_specs=[pl.BlockSpec((rows, n_ex), lambda i: (i, 0))] * n_dp
        + [fixed(x) for x in seen]
        + [fixed(x) for x in users]
        + [
            pl.BlockSpec((rows, width), lambda i: (jnp.minimum(i, last), 0)),
            pl.BlockSpec((n_ex, width), lambda i: (0, 0)),
        ],
        out_specs=[
            pl.BlockSpec((rows, width), lambda i: (i, 0)),
            pl.BlockSpec((n_ex, width), lambda i: (0, 0)),
            pl.BlockSpec((1, width), lambda i: (0, 0)),
        ],
        out_shape=[
            jax.ShapeDtypeStruct((n_items, width), jnp.float32),
            jax.ShapeDtypeStruct((n_ex, width), jnp.float32),
            jax.ShapeDtypeStruct((1, width), jnp.float32),
        ],
        cost_estimate=pl.CostEstimate(
            flops=2 * n_dp * n_items * n_ex * width,
            transcendentals=n_ex,
            bytes_accessed=4 * n_dp * n_items * n_ex,
        ),
        name="middle",
    )(*expos, *seen, *users, users[0], items)


def exchange(x):
    return lax.all_to_all(x, AXES, split_axis=0, concat_axis=0, tiled=True)


def fetch(blocks, axis):
    n = lax.axis_size(axis)
    return [blocks[0]] + [
        lax.ppermute(blocks[k], axis, [((i + k) % n, i) for i in range(n)]) for k in range(1, n)
    ]


def give(blocks, axis):
    n = lax.axis_size(axis)
    return [blocks[0]] + [
        lax.ppermute(blocks[k], axis, [(i, (i + k) % n) for i in range(n)]) for k in range(1, n)
    ]


def per_device(
    id_table, ada_state, user_first, user_second, item_first, item_second, fetch_rows, lookup_slots
):
    width = id_table.shape[1]
    n_dp = lax.axis_size("dp")
    n_all = n_dp * lax.axis_size("shard")
    cap = fetch_rows.shape[-1]
    n_ex = EXAMPLES_ON_CHIP
    asked = exchange(fetch_rows.reshape(n_all, cap))
    fetched = id_table.at[asked.reshape(-1)].get(mode="promise_in_bounds")
    slot_rows = exchange(fetched.reshape(n_all, cap, width)).reshape(-1, width)
    slot_index = lookup_slots[0]
    looked = slot_rows.at[slot_index].get(mode="promise_in_bounds")

    user_vec, user_saved = tower(looked[:n_ex], user_first, user_second)
    user_bf = user_vec.astype(jnp.bfloat16)
    item_rows, user_bf = lax.optimization_barrier((looked[n_ex:], user_bf))
    group_users = fetch([user_bf] * n_dp, "dp")
    item_vec, item_saved = tower(item_rows, item_first, item_second)
    item_bf = item_vec.astype(jnp.bfloat16)

    parts, pulls, expos = [], [], []
    for block in group_users:
        expo = jnp.exp(
            jnp.dot(item_bf, block.T, preferred_element_type=jnp.float32) / logit_divisor
        )
        parts.append(jnp.sum(expo, axis=0))
        pulls.append(
            lax.dot_general(
                expo.astype(jnp.bfloat16),
                item_bf,
                (((0,), (0,)), ((), ())),
                preferred_element_type=jnp.float32,
            )
        )
        expos.append(expo)
    mine = jnp.stack(parts)
    seen = fetch([mine] * n_dp, "dp")
    returned = give([pulls[0]] + [p.astype(jnp.bfloat16) for p in pulls[1:]], "dp")
    item_cot, share, loss_row = middle(expos, seen, group_users, item_bf)
    positive = item_bf[:n_ex].astype(jnp.float32)

    item_look, item_sums = tower_back(item_saved, item_cot)
    pulled = sum(p.astype(jnp.float32) for p in returned)
    user_cot = (pulled * share - positive) / logit_divisor
    sent = exchange(
        tower_back(
            user_saved, user_cot, (item_look, item_sums, lookup_slots, loss_row), n_all, cap
        )
    )
    deep = sent.shape[1] - cap - 8
    chunk = jnp.sum(sent[:, : deep + 8].astype(jnp.float32), axis=0)
    mean_loss = jnp.sum(chunk[deep, :3]) / (n_all * n_ex)
    chunk = (chunk[:deep] / n_all).astype(jnp.bfloat16)
    row = jnp.stack(fetch([chunk] * lax.axis_size("shard"), "shard"))
    outs = spread(fetch([row] * n_dp, "dp"), (user_first, user_second, item_first, item_second))

    new_table, new_state = update(id_table, ada_state, asked.reshape(n_all, 1, cap), sent)
    return (new_table, new_state, *outs, mean_loss)


def solution(mesh):
    return jax.shard_map(
        per_device,
        mesh=mesh,
        in_specs=(
            P(("dp", "shard"), None),
            P(("dp", "shard")),
            P(),
            P(),
            P(),
            P(),
            P(("dp", "shard"), None, None, None),
            P(("dp", "shard"), None),
        ),
        out_specs=(P(("dp", "shard"), None), P(("dp", "shard")), P(), P(), P(), P(), P()),
        check_vma=False,
    )
```

time: 195 us -> 173 us (0.89)
  other arithmetic: 40.9 us -> 3.22 us
  Pallas kernels: 0 us -> 34.1 us
  matrix products: 33.2 us -> 7.57 us
  starting transfers between devices: 14.1 us -> 20.6 us
  waiting for transfers between devices: 35.8 us -> 41 us
  between operations: 7.1 us -> 3.01 us
    pallas_call x0 -> x5, Pallas kernels: none -> 34.1 us  [the longest x2 14.6 us: tower_back(): pl.pallas_call(functools.partial(back_kernel, last), grid=(n // rows,), i...]
    dot_general x24 -> x12, matrix products: 33.2 us -> 7.57 us  [the longest x4 3.83 us: product(): lax.dot_general(a, b, (dims, ((), ())), precision=fine, preferred_element...]
    scatter-add x2 -> x0, other arithmetic: 25.3 us -> none  [the longest x1 15.7 us: per_device(): grad_rows = jnp.zeros_like(id_table).at[asked.reshape(-1)].add(sent[:, :c...]
    ppermute x9 -> x19, starting transfers between devices: 8.74 us -> 17.9 us  [the longest x16 14.8 us: fetch(): lax.ppermute(blocks[k], axis, [((i + k) % n, i) for i in range(n)])]
    ppermute x9 -> x19, waiting for transfers between devices: 5.62 us -> 10.7 us  [the longest x16 10.7 us: fetch(): lax.ppermute(blocks[k], axis, [((i + k) % n, i) for i in range(n)])]
    reduce_sum x6 -> x2, other arithmetic: 4.98 us -> 0.69 us  [the longest x1 0.6 us: per_device(): mean_loss = jnp.sum(chunk[deep, :3]) / (n_all * n_ex)]
    sub x2 -> x0, other arithmetic: 4.27 us -> none  [the longest x1 4.22 us: per_device(): id_table - learn_rate * grad_rows / (jnp.sqrt(new_state)[:, None] + epsilon)]
    all_to_all x2 -> x1, starting transfers between devices: 5.39 us -> 2.79 us  [exchange(): return lax.all_to_all(x, AXES, split_axis=0, concat_axis=0, tiled=True)]
  transfers between devices with their start and end apart: 11 -> 20, of which waited for: 2 -> 7; matrix products, arithmetic and copies ran while one was open for 24% -> 3% of each run, Pallas kernels for 0% -> 14%
where the time goes in v2:
time: 173 us; the launch traced here: 172 us
  blocking collectives  47.8 us (28%)
  waiting for transfers between devices  41 us (24%)
  Pallas kernels  34.1 us (20%)
  starting transfers between devices  20.6 us (12%)
  local copies, waits for them, and re-layouts  14.9 us (9%)
  matrix products  7.57 us (4%)
  other arithmetic  3.22 us (2%)
  between operations  3.01 us (2%)
    all_to_all x2, blocking collectives, exchange(): return lax.all_to_all(x, AXES, split_axis=0, concat_axis=0, tiled=True)  47.8 us
    all_to_all x1, waiting for transfers between devices, exchange(): return lax.all_to_all(x, AXES, split_axis=0, concat_axis=0, tiled=True)  30.2 us
    ppermute x16, starting transfers between devices, fetch(): lax.ppermute(blocks[k], axis, [((i + k) % n, i) for i in range(n)])  14.8 us
    pallas_call x2, Pallas kernels, tower_back(): pl.pallas_call(functools.partial(back_kernel, last), grid=(n // rows,), i...  14.6 us
    pallas_call x1, Pallas kernels, update(): pl.pallas_call(functools.partial(update_kernel, skip), grid_spec=pltpu.Pr...  11 us
    ppermute x16, waiting for transfers between devices, fetch(): lax.ppermute(blocks[k], axis, [((i + k) % n, i) for i in range(n)])  10.7 us
    gather x1, local copies, waits for them, and re-layouts, per_device(): fetched = id_table.at[asked.reshape(-1)].get(mode='promise_in_bounds')  7.28 us
    pallas_call x1, Pallas kernels, middle(): pl.pallas_call(functools.partial(middle_kernel, n_dp, n_ex), grid=(n_item...  6.41 us
  transfers between devices with their start and end apart: 20, of which 7 were waited for; matrix products, arithmetic and copies ran while one was open for 3% of the time, Pallas kernels for 14%

profile of v2, /device:TPU:0, one launch (start us, length us, event | category | flops | bytes accessed | tf_op | source)
XLA Modules:
  0.0 172.3 jit_solution(2677140833961395442)
XLA Ops:
  0.6 14.4 %all_to_all.19.rows_ref = s32[32,1,72]{2,1,0:T(1,128)S(1)} all-to-all(s32[32,1,72]{2,1,0:T(1,128)} %bitcast.48), channel_id=1, replica_groups=mesh['dp'=4,'shard'=8] {'dp','shard'}, dimensions={0} | all-to-all | bytes 18432 | tf_op jit(solution)/shard_map/all_to_all | solution.py:340
  16.4 7.3 %gather_fusion = f32[2304,128]{1,0:T(8,128)} fusion(f32[8192,128]{1,0:T(8,128)} %table.1, s32[3072]{0:T(1024)S(1)} %pad_clamp_fusion), kind=kCustom, calls=%fused_computation | custom fusion | bytes 2368512 | tf_op jit(solution)/shard_map/gather | solution.py:366
  23.7 2.8 %all-to-all-start.1 = ((f32[32,72,128]{2,1,0:T(8,128)}), f32[32,72,128]{2,1,0:T(8,128)S(1)}, u32[]{:S(2)}, u32[]{:S(2)}) async-start(f32[32,72,128]{2,1,0:T(8,128)} %bitcast.1), calls=%async_computation.1 | async-start | bytes 2359296 | tf_op jit(solution)/shard_map/all_to_all | solution.py:340
  26.6 30.2 %all-to-all-done.1 = f32[32,72,128]{2,1,0:T(8,128)S(1)} async-done(((f32[32,72,128]{2,1,0:T(8,128)}), f32[32,72,128]{2,1,0:T(8,128)S(1)}, u32[]{:S(2)}, u32[]{:S(2)}) %all-to-all-start.1) | async-done | bytes 1179680 | tf_op jit(solution)/shard_map/all_to_all | solution.py:340
  56.8 2.6 %gather_fusion.1 = f32[1536,128]{1,0:T(8,128)S(1)} fusion(f32[2304,128]{1,0:T(8,128)S(1)} %bitcast.46, s32[2048]{0:T(1024)S(1)} %pad_clamp_fusion.1), kind=kCustom, calls=%fused_computation.1 | custom fusion | bytes 1579008 | tf_op jit(solution)/shard_map/gather | solution.py:369
  62.7 1.5 multiply_reduce_fusion
  67.7 1.5 collective-permute-start.4
  70.1 5.3 %collective-permute-done.2.refs_10_ = bf16[512,128]{1,0:T(8,128)(2,1)S(1)} collective-permute-done((bf16[512,128]{1,0:T(8,128)(2,1)S(1)}, bf16[512,128]{1,0:T(8,128)(2,1)S(1)}, u32[]{:S(2)}, u32[]{:S(2)}) %collective-permute-start.2) | collective-permute-done | bytes 131104 | tf_op jit(solution)/shard_map/ppermute | solution.py:346
  76.5 1.4 collective-permute-start.7
  77.9 1.9 %collective-permute-start.8 = (f32[4,512]{1,0:T(4,128)S(1)}, f32[4,512]{1,0:T(4,128)S(1)}, u32[]{:S(2)}, u32[]{:S(2)}) collective-permute-start(f32[4,512]{1,0:T(4,128)S(1)} %pad_maximum_fusion.refs_4_), channel_id=1, source_target_pairs={{24,0},{0,8},{8,16},{16,24},{25,1},{1,9},{9,17},{17,25},{26,2},{2,... | collective-permute-start | bytes 24584 | tf_op jit(solution)/shard_map/ppermute | solution.py:346
  80.4 1.0 collective-permute-start.5
  83.2 1.3 collective-permute-start.1
  85.7 6.4 %middle.1 = (f32[1024,128]{1,0:T(8,128)}, f32[512,128]{1,0:T(8,128)}, f32[1,128]{1,0:T(1,128)}) custom-call(f32[1024,512]{1,0:T(8,128)} %copy-done.2, f32[1024,512]{1,0:T(8,128)} %copy-done.3, f32[1024,512]{1,0:T(8,128)} %copy-done.4, f32[1024,512]{1,0:T(8,128)} %copy-done.5, f32[4,512]{1,0:T(4,128)} %copy-done.25, f32[4,512]{1,0:T(4,128)} %copy-done.27, ...), custom_call_target="tpu_custom_call" | custom-call | flops 536870912 | bytes 8388608 | tf_op jit(solution)/shard_map/middle/pallas_call | solution.py:310
  92.1 7.4 %item_back.1 = (bf16[1024,128]{1,0:T(8,128)(2,1)}, bf16[1024,128]{1,0:T(8,128)(2,1)}) custom-call(f32[1024,128]{1,0:T(8,128)} %copy-done.12, f32[1024,512]{1,0:T(8,128)} %copy-done.10, f32[1024,128]{1,0:T(8,128)} %copy-done.11, f32[1024,128]{1,0:T(8,128)} %get-tuple-element.23.refs_3_, f32[128,512]{1,0:T(8,128)} %refs_4_.2, f32[512,128]{1,0:T(8,128)} %refs_5_.2), custom_call_target="tpu_custom_call" | custom-call | flops 1610612736 | bytes 4194304 | tf_op jit(solution)/shard_map/item_back/pallas_call | solution.py:141
  100.3 7.2 %user_back.1 = bf16[32,144,128]{2,1,0:T(8,128)(2,1)} custom-call(f32[512,128]{1,0:T(8,128)} %slice.28.refs_0_, f32[512,512]{1,0:T(8,128)} %copy-done.7, f32[512,128]{1,0:T(8,128)} %copy-done.8, f32[512,128]{1,0:T(8,128)} %subtract_multiply_fusion.refs_3_, f32[128,512]{1,0:T(8,128)} %refs_4_.3, f32[512,128]{1,0:T(8,128)} %refs_5_.3, ...), custom_call_target="tpu_custom_call" | custom-call | flops 805306368 | bytes 2097152 | tf_op jit(solution)/shard_map/user_back/pallas_call | solution.py:141
  107.5 33.4 %all_to_all.20.grads = bf16[32,144,128]{2,1,0:T(8,128)(2,1)S(1)} all-to-all(bf16[32,144,128]{2,1,0:T(8,128)(2,1)} %user_back.1), channel_id=1, replica_groups=mesh['dp'=4,'shard'=8] {'dp','shard'}, dimensions={0} | all-to-all | bytes 2359296 | tf_op jit(solution)/shard_map/all_to_all | solution.py:340
  141.0 1.2 collective-permute-start.9
  142.8 2.1 %collective-permute-start.12 = (bf16[64,128]{1,0:T(8,128)(2,1)S(1)}, bf16[64,128]{1,0:T(8,128)(2,1)S(1)}, u32[]{:S(2)}, u32[]{:S(2)}) collective-permute-start(bf16[64,128]{1,0:T(8,128)(2,1)S(1)} %get-tuple-element.34), channel_id=1, source_target_pairs={{4,0},{5,1},{6,2},{7,3},{0,4},{1,5},{2,6},{3,7},{12,8},{13,9},{14,... | collective-permute-start | bytes 49160 | tf_op jit(solution)/shard_map/ppermute | solution.py:346
  145.8 1.2 collective-permute-start.14
  147.4 1.5 collective-permute-done.13
  149.0 2.3 %collective-permute-done.14 = bf16[64,128]{1,0:T(8,128)(2,1)S(1)} collective-permute-done((bf16[64,128]{1,0:T(8,128)(2,1)S(1)}, bf16[64,128]{1,0:T(8,128)(2,1)S(1)}, u32[]{:S(2)}, u32[]{:S(2)}) %collective-permute-start.14) | collective-permute-done | bytes 16416 | tf_op jit(solution)/shard_map/ppermute | solution.py:346
  152.8 1.4 collective-permute-start.17
  156.6 11.0 %update.1 = (f32[8192,128]{1,0:T(8,128)}, f32[64,128]{1,0:T(8,128)}) custom-call(s32[32,1,72]{2,1,0:T(1,128)} %copy-done.21, bf16[32,144,128]{2,1,0:T(8,128)(2,1)} %copy-done.6, f32[8192,128]{1,0:T(8,128)} %table.1, f32[64,128]{1,0:T(8,128)} %bitcast.47), custom_call_target="tpu_custom_call" | custom-call | flops 20971520 | bytes 8388608 | tf_op jit(solution)/shard_map/update/pallas_call | solution.py:199
  169.0 2.2 %spread.1 = (f32[128,512]{1,0:T(8,128)}, f32[512,128]{1,0:T(8,128)}, f32[128,512]{1,0:T(8,128)}, f32[512,128]{1,0:T(8,128)}) custom-call(s32[2]{0:T(128)} %pad_add_fusion.place, bf16[8,64,128]{2,1,0:T(8,128)(2,1)} %copy-done.20, bf16[8,64,128]{2,1,0:T(8,128)(2,1)} %copy-done.22, bf16[8,64,128]{2,1,0:T(8,128)(2,1)} %copy-done.23, bf16[8,64,128]{2,1,0:T(8,128)(2,1)} %copy-done.24), custom_call_target="tpu_custom_call" | custom-call | flops 262144 | bytes 1572864 | tf_op jit(solution)/shard_map/spread/pallas_call | solution.py:249
  (127 shorter events, 20.8 us)
Async XLA Ops:
  23.7 33.1 %all-to-all-start.1 = ((f32[32,72,128]{2,1,0:T(8,128)}), f32[32,72,128]{2,1,0:T(8,128)S(1)}, u32[]{:S(2)}, u32[]{:S(2)}) async-start(f32[32,72,128]{2,1,0:T(8,128)} %bitcast.1), calls=%async_computation.1 | async-start | bytes 2359296 | tf_op jit(solution)/shard_map/all_to_all | solution.py:340
  64.5 5.2 %collective-permute-start = (bf16[512,128]{1,0:T(8,128)(2,1)S(1)}, bf16[512,128]{1,0:T(8,128)(2,1)S(1)}, u32[]{:S(2)}, u32[]{:S(2)}) collective-permute-start(bf16[512,128]{1,0:T(8,128)(2,1)S(1)} %divide_convert_fusion.1.refs_8_.refs_12_), channel_id=1, source_target_pairs={{8,0},{16,8},{24,16},{0,24},{9,1},{17,9},{25,17},{1,25},{10,2},{18... | collective-permute-start | bytes 393224 | tf_op jit(solution)/shard_map/ppermute | solution.py:346
  65.3 17.4 %copy-start = (bf16[1024,128]{1,0:T(8,128)(2,1)}, bf16[1024,128]{1,0:T(8,128)(2,1)S(1)}, u32[]{:S(2)}) copy-start(bf16[1024,128]{1,0:T(8,128)(2,1)S(1)} %divide_convert_fusion.refs_13_) | copy-start | bytes 786436
  67.1 8.3 %collective-permute-start.2 = (bf16[512,128]{1,0:T(8,128)(2,1)S(1)}, bf16[512,128]{1,0:T(8,128)(2,1)S(1)}, u32[]{:S(2)}, u32[]{:S(2)}) collective-permute-start(bf16[512,128]{1,0:T(8,128)(2,1)S(1)} %divide_convert_fusion.1.refs_8_.refs_12_), channel_id=1, source_target_pairs={{16,0},{24,8},{0,16},{8,24},{17,1},{25,9},{1,17},{9,25},{18,2},{26... | collective-permute-start | bytes 393224 | tf_op jit(solution)/shard_map/ppermute | solution.py:346
  67.7 8.2 %collective-permute-start.4 = (bf16[512,128]{1,0:T(8,128)(2,1)S(1)}, bf16[512,128]{1,0:T(8,128)(2,1)S(1)}, u32[]{:S(2)}, u32[]{:S(2)}) collective-permute-start(bf16[512,128]{1,0:T(8,128)(2,1)S(1)} %divide_convert_fusion.1.refs_8_.refs_12_), channel_id=1, source_target_pairs={{24,0},{0,8},{8,16},{16,24},{25,1},{1,9},{9,17},{17,25},{26,2},{2,... | collective-permute-start | bytes 393224 | tf_op jit(solution)/shard_map/ppermute | solution.py:346
  70.1 12.5 %copy-start.3 = (f32[1024,512]{1,0:T(8,128)}, f32[1024,512]{1,0:T(8,128)S(1)}, u32[]{:S(2)}) copy-start(f32[1024,512]{1,0:T(8,128)S(1)} %get-tuple-element.44.refs_1_) | copy-start | bytes 6291460
  76.4 6.7 %collective-permute-start.6 = (f32[4,512]{1,0:T(4,128)S(1)}, f32[4,512]{1,0:T(4,128)S(1)}, u32[]{:S(2)}, u32[]{:S(2)}) collective-permute-start(f32[4,512]{1,0:T(4,128)S(1)} %pad_maximum_fusion.refs_4_), channel_id=1, source_target_pairs={{8,0},{16,8},{24,16},{0,24},{9,1},{17,9},{25,17},{1,25},{10,2},{18... | collective-permute-start | bytes 24584 | tf_op jit(solution)/shard_map/ppermute | solution.py:346
  76.5 8.0 %collective-permute-start.7 = (f32[4,512]{1,0:T(4,128)S(1)}, f32[4,512]{1,0:T(4,128)S(1)}, u32[]{:S(2)}, u32[]{:S(2)}) collective-permute-start(f32[4,512]{1,0:T(4,128)S(1)} %pad_maximum_fusion.refs_4_), channel_id=1, source_target_pairs={{16,0},{24,8},{0,16},{8,24},{17,1},{25,9},{1,17},{9,25},{18,2},{26... | collective-permute-start | bytes 24584 | tf_op jit(solution)/shard_map/ppermute | solution.py:346
  77.9 6.6 %collective-permute-start.8 = (f32[4,512]{1,0:T(4,128)S(1)}, f32[4,512]{1,0:T(4,128)S(1)}, u32[]{:S(2)}, u32[]{:S(2)}) collective-permute-start(f32[4,512]{1,0:T(4,128)S(1)} %pad_maximum_fusion.refs_4_), channel_id=1, source_target_pairs={{24,0},{0,8},{8,16},{16,24},{25,1},{1,9},{9,17},{17,25},{26,2},{2,... | collective-permute-start | bytes 24584 | tf_op jit(solution)/shard_map/ppermute | solution.py:346
  80.4 19.1 %collective-permute-start.5 = (bf16[512,128]{1,0:T(8,128)(2,1)S(1)}, bf16[512,128]{1,0:T(8,128)(2,1)S(1)}, u32[]{:S(2)}, u32[]{:S(2)}) collective-permute-start(bf16[512,128]{1,0:T(8,128)(2,1)S(1)} %convolution_convert_fusion), channel_id=1, source_target_pairs={{0,24},{8,0},{16,8},{24,16},{1,25},{9,1},{17,9},{25,17},{2,26},{10... | collective-permute-start | bytes 393224 | tf_op jit(solution)/shard_map/ppermute | solution.py:353
  81.9 17.6 %collective-permute-start.3 = (bf16[512,128]{1,0:T(8,128)(2,1)S(1)}, bf16[512,128]{1,0:T(8,128)(2,1)S(1)}, u32[]{:S(2)}, u32[]{:S(2)}) collective-permute-start(bf16[512,128]{1,0:T(8,128)(2,1)S(1)} %convolution_convert_fusion.1), channel_id=1, source_target_pairs={{0,16},{8,24},{16,0},{24,8},{1,17},{9,25},{17,1},{25,9},{2,18},{10... | collective-permute-start | bytes 393224 | tf_op jit(solution)/shard_map/ppermute | solution.py:353
  83.2 16.3 %collective-permute-start.1 = (bf16[512,128]{1,0:T(8,128)(2,1)S(1)}, bf16[512,128]{1,0:T(8,128)(2,1)S(1)}, u32[]{:S(2)}, u32[]{:S(2)}) collective-permute-start(bf16[512,128]{1,0:T(8,128)(2,1)S(1)} %convolution_convert_fusion.2), channel_id=1, source_target_pairs={{0,8},{8,16},{16,24},{24,0},{1,9},{9,17},{17,25},{25,1},{2,10},{10... | collective-permute-start | bytes 393224 | tf_op jit(solution)/shard_map/ppermute | solution.py:353
  140.9 15.7 %copy-start.6 = (bf16[32,144,128]{2,1,0:T(8,128)(2,1)}, bf16[32,144,128]{2,1,0:T(8,128)(2,1)S(1)}, u32[]{:S(2)}) copy-start(bf16[32,144,128]{2,1,0:T(8,128)(2,1)S(1)} %all_to_all.20.grads) | copy-start | bytes 3538948
  141.0 4.8 %collective-permute-start.9 = (bf16[64,128]{1,0:T(8,128)(2,1)S(1)}, bf16[64,128]{1,0:T(8,128)(2,1)S(1)}, u32[]{:S(2)}, u32[]{:S(2)}) collective-permute-start(bf16[64,128]{1,0:T(8,128)(2,1)S(1)} %get-tuple-element.34), channel_id=1, source_target_pairs={{1,0},{2,1},{3,2},{4,3},{5,4},{6,5},{7,6},{0,7},{9,8},{10,9},{11,1... | collective-permute-start | bytes 49160 | tf_op jit(solution)/shard_map/ppermute | solution.py:346
  142.2 4.8 %collective-permute-start.10 = (bf16[64,128]{1,0:T(8,128)(2,1)S(1)}, bf16[64,128]{1,0:T(8,128)(2,1)S(1)}, u32[]{:S(2)}, u32[]{:S(2)}) collective-permute-start(bf16[64,128]{1,0:T(8,128)(2,1)S(1)} %get-tuple-element.34), channel_id=1, source_target_pairs={{2,0},{3,1},{4,2},{5,3},{6,4},{7,5},{0,6},{1,7},{10,8},{11,9},{12,... | collective-permute-start | bytes 49160 | tf_op jit(solution)/shard_map/ppermute | solution.py:346
  142.8 4.3 %collective-permute-start.11 = (bf16[64,128]{1,0:T(8,128)(2,1)S(1)}, bf16[64,128]{1,0:T(8,128)(2,1)S(1)}, u32[]{:S(2)}, u32[]{:S(2)}) collective-permute-start(bf16[64,128]{1,0:T(8,128)(2,1)S(1)} %get-tuple-element.34), channel_id=1, source_target_pairs={{3,0},{4,1},{5,2},{6,3},{7,4},{0,5},{1,6},{2,7},{11,8},{12,9},{13,... | collective-permute-start | bytes 49160 | tf_op jit(solution)/shard_map/ppermute | solution.py:346
  142.8 4.6 %collective-permute-start.12 = (bf16[64,128]{1,0:T(8,128)(2,1)S(1)}, bf16[64,128]{1,0:T(8,128)(2,1)S(1)}, u32[]{:S(2)}, u32[]{:S(2)}) collective-permute-start(bf16[64,128]{1,0:T(8,128)(2,1)S(1)} %get-tuple-element.34), channel_id=1, source_target_pairs={{4,0},{5,1},{6,2},{7,3},{0,4},{1,5},{2,6},{3,7},{12,8},{13,9},{14,... | collective-permute-start | bytes 49160 | tf_op jit(solution)/shard_map/ppermute | solution.py:346
  144.9 4.1 %collective-permute-start.13 = (bf16[64,128]{1,0:T(8,128)(2,1)S(1)}, bf16[64,128]{1,0:T(8,128)(2,1)S(1)}, u32[]{:S(2)}, u32[]{:S(2)}) collective-permute-start(bf16[64,128]{1,0:T(8,128)(2,1)S(1)} %get-tuple-element.34), channel_id=1, source_target_pairs={{5,0},{6,1},{7,2},{0,3},{1,4},{2,5},{3,6},{4,7},{13,8},{14,9},{15,... | collective-permute-start | bytes 49160 | tf_op jit(solution)/shard_map/ppermute | solution.py:346
  145.8 5.5 %collective-permute-start.14 = (bf16[64,128]{1,0:T(8,128)(2,1)S(1)}, bf16[64,128]{1,0:T(8,128)(2,1)S(1)}, u32[]{:S(2)}, u32[]{:S(2)}) collective-permute-start(bf16[64,128]{1,0:T(8,128)(2,1)S(1)} %get-tuple-element.34), channel_id=1, source_target_pairs={{6,0},{7,1},{0,2},{1,3},{2,4},{3,5},{4,6},{5,7},{14,8},{15,9},{8,1... | collective-permute-start | bytes 49160 | tf_op jit(solution)/shard_map/ppermute | solution.py:346
  147.0 5.0 %collective-permute-start.15 = (bf16[64,128]{1,0:T(8,128)(2,1)S(1)}, bf16[64,128]{1,0:T(8,128)(2,1)S(1)}, u32[]{:S(2)}, u32[]{:S(2)}) collective-permute-start(bf16[64,128]{1,0:T(8,128)(2,1)S(1)} %get-tuple-element.34), channel_id=1, source_target_pairs={{7,0},{0,1},{1,2},{2,3},{3,4},{4,5},{5,6},{6,7},{15,8},{8,9},{9,10... | collective-permute-start | bytes 49160 | tf_op jit(solution)/shard_map/ppermute | solution.py:346
  152.0 15.6 %copy-start.20 = (bf16[8,64,128]{2,1,0:T(8,128)(2,1)}, bf16[8,64,128]{2,1,0:T(8,128)(2,1)S(1)}, u32[]{:S(2)}) copy-start(bf16[8,64,128]{2,1,0:T(8,128)(2,1)S(1)} %constant_dynamic-update-slice_fusion.refs_0_) | copy-start | bytes 393220
  152.0 15.6 %collective-permute-start.16 = (bf16[8,64,128]{2,1,0:T(8,128)(2,1)S(1)}, bf16[8,64,128]{2,1,0:T(8,128)(2,1)S(1)}, u32[]{:S(2)}, u32[]{:S(2)}) collective-permute-start(bf16[8,64,128]{2,1,0:T(8,128)(2,1)S(1)} %constant_dynamic-update-slice_fusion.refs_0_), channel_id=1, source_target_pairs={{8,0},{16,8},{24,16},{0,24},{9,1},{17,9},{25,17},{1,25},{10,2},{18... | collective-permute-start | bytes 393224 | tf_op jit(solution)/shard_map/ppermute | solution.py:346
  152.8 14.8 %collective-permute-start.17 = (bf16[8,64,128]{2,1,0:T(8,128)(2,1)S(1)}, bf16[8,64,128]{2,1,0:T(8,128)(2,1)S(1)}, u32[]{:S(2)}, u32[]{:S(2)}) collective-permute-start(bf16[8,64,128]{2,1,0:T(8,128)(2,1)S(1)} %constant_dynamic-update-slice_fusion.refs_0_), channel_id=1, source_target_pairs={{16,0},{24,8},{0,16},{8,24},{17,1},{25,9},{1,17},{9,25},{18,2},{26... | collective-permute-start | bytes 393224 | tf_op jit(solution)/shard_map/ppermute | solution.py:346
  154.2 13.5 %collective-permute-start.18 = (bf16[8,64,128]{2,1,0:T(8,128)(2,1)S(1)}, bf16[8,64,128]{2,1,0:T(8,128)(2,1)S(1)}, u32[]{:S(2)}, u32[]{:S(2)}) collective-permute-start(bf16[8,64,128]{2,1,0:T(8,128)(2,1)S(1)} %constant_dynamic-update-slice_fusion.refs_0_), channel_id=1, source_target_pairs={{24,0},{0,8},{8,16},{16,24},{25,1},{1,9},{9,17},{17,25},{26,2},{2,... | collective-permute-start | bytes 393224 | tf_op jit(solution)/shard_map/ppermute | solution.py:346
  (27 other events, 84.7 us)

commit v3 on v2

--- a/solution.py
+++ b/solution.py
@@ -7,6 +7,7 @@
 from jax.experimental.pallas import tpu as pltpu
 from jax.sharding import PartitionSpec as P
 
+
 EXAMPLES_ON_CHIP = 512
 AXES = ("dp", "shard")
 
@@ -28,7 +29,7 @@
     active = hidden * gate
     out = product(active, second_w, ((1,), (0,)))
     norm = jnp.sqrt(jnp.sum(out * out, axis=1, keepdims=True) + 1e-06)
-    return out / norm, (looked, hidden, out, first_w, second_w)
+    return out / norm, (hidden, out, first_w, second_w)
 
 
 def halves(x):
@@ -113,11 +114,11 @@
                 sent[k + j, deep + 8 :, :] = total[j * cap : (j + 1) * cap].astype(sent.dtype)
 
 
-def tower_back(saved, cot, rest=(), n_all=0, cap=0):
-    looked, hidden, out, first_w, second_w = saved
-    n, width = looked.shape
+def tower_back(looked, start, saved, cot, rest=(), n_all=0, cap=0):
+    hidden, out, first_w, second_w = saved
+    n, width = out.shape
     inner = hidden.shape[1]
-    rows = min(n, 256)
+    rows = min(n, 512)
     last = bool(rest)
 
     def by_rows(w):
@@ -141,7 +142,8 @@
     return pl.pallas_call(
         functools.partial(back_kernel, last),
         grid=(n // rows,),
-        in_specs=[by_rows(width), by_rows(inner), by_rows(width), by_rows(width)]
+        in_specs=[pl.BlockSpec((rows, width), lambda i: (i + start // rows, 0))]
+        + [by_rows(inner), by_rows(width), by_rows(width)]
         + [fixed(x.shape) for x in (first_w, second_w, *rest)],
         out_specs=out_specs,
         out_shape=out_shape,
@@ -224,77 +226,68 @@
     return new_table, new_state.reshape(-1)
 
 
-def spread_kernel(place, *refs):
-    n_dp = len(refs) - 5
-    pieces, outs, whole = refs[:n_dp], refs[n_dp:-1], refs[-1]
-    n_sh, rows, width = pieces[0].shape
-    for k, piece in enumerate(pieces):
-        for j in range(n_sh):
-            d = lax.rem(place[0] + k, n_dp)
-            s = lax.rem(place[1] + j, n_sh)
-            at = pl.multiple_of((d * n_sh + s) * rows, rows)
-            whole[pl.ds(at, rows), :] = piece[j].astype(jnp.float32)
+def spread_kernel(whole, *outs):
     at = 0
     for first, second in (outs[:2], outs[2:]):
+        width = second.shape[1]
         for c in range(0, first.shape[1], width):
-            first[:, c : c + width] = whole[at : at + width, :]
+            first[:, c : c + width] = whole[at : at + width, :].astype(first.dtype)
             at += width
-        second[...] = whole[at : at + second.shape[0], :]
+        second[...] = whole[at : at + second.shape[0], :].astype(second.dtype)
         at += second.shape[0]
 
 
-def spread(pieces, weights):
-    place = jnp.stack([lax.axis_index("dp"), lax.axis_index("shard")]).astype(jnp.int32)
-    total = sum(w.size for w in weights)
+def spread(whole, weights):
     return pl.pallas_call(
         spread_kernel,
-        in_specs=[pl.BlockSpec(memory_space=pltpu.SMEM)]
-        + [pl.BlockSpec(memory_space=pltpu.VMEM)] * len(pieces),
-        out_specs=[pl.BlockSpec(memory_space=pltpu.VMEM)] * 4,
-        out_shape=[jax.ShapeDtypeStruct(w.shape, jnp.float32) for w in weights],
-        scratch_shapes=[
-            pltpu.VMEM((total // pieces[0].shape[-1], pieces[0].shape[-1]), jnp.float32)
-        ],
-        cost_estimate=pl.CostEstimate(flops=total, transcendentals=0, bytes_accessed=6 * total),
+        in_specs=[pl.BlockSpec(memory_space=pltpu.VMEM)],
+        out_specs=[pl.BlockSpec(memory_space=pltpu.VMEM)] * len(weights),
+        out_shape=[jax.ShapeDtypeStruct(w.shape, w.dtype) for w in weights],
+        cost_estimate=pl.CostEstimate(
+            flops=whole.size, transcendentals=0, bytes_accessed=6 * whole.size
+        ),
         name="spread",
-    )(place, *pieces)
+    )(whole)
 
 
 def middle_kernel(n_dp, n_ex, *refs):
     expos, seen, users = refs[:n_dp], refs[n_dp : 2 * n_dp], refs[2 * n_dp : 3 * n_dp]
-    own, positive, item_cot, share, loss_row = refs[3 * n_dp :]
+    own, positive, item_cot, share, loss_row, scaled = refs[3 * n_dp :]
     step = pl.program_id(0)
-    totals = []
-    for b in range(n_dp):
-        total = seen[0][b : b + 1, :]
-        for k in range(1, n_dp):
-            j = (b - k) % n_dp
-            total = total + seen[k][j : j + 1, :]
-        totals.append(total)
-    acc = jnp.zeros(item_cot.shape, jnp.float32)
-    for expo, total, user in zip(expos, totals, users):
-        probs = (expo[...] * (1.0 / total)).astype(jnp.bfloat16)
-        acc = acc + jnp.dot(probs, user[...], preferred_element_type=jnp.float32)
-    rows = item_cot.shape[0]
-    own_f = own[...].astype(jnp.float32)
-    acc = acc - jnp.where(step * rows < n_ex, own_f, jnp.zeros_like(own_f))
-    item_cot[...] = acc / logit_divisor
+    width = share.shape[1]
 
     @pl.when(step == 0)
     def _():
-        width = share.shape[1]
-        share[...] = jnp.broadcast_to(1.0 / totals[0], (width, n_ex)).T
-        pairs = users[0][...].astype(jnp.float32) * positive[...].astype(jnp.float32)
-        score = jnp.sum(jnp.sum(pairs, axis=0, keepdims=True), axis=1, keepdims=True)
-        loss = jnp.sum(jnp.log(totals[0]), axis=1, keepdims=True) - score / logit_divisor
-        rest = jnp.broadcast_to(loss, loss_row.shape)
-        lane = lax.broadcasted_iota(jnp.int32, loss_row.shape, 1)
-        row = jnp.zeros(loss_row.shape, jnp.float32)
-        for k in range(3):
-            term = rest.astype(jnp.bfloat16).astype(jnp.float32)
-            row = jnp.where(lane == k, term, row)
-            rest = rest - term
-        loss_row[...] = row
+        for b in range(n_dp):
+            total = seen[0][b : b + 1, :]
+            for k in range(1, n_dp):
+                j = (b - k) % n_dp
+                total = total + seen[k][j : j + 1, :]
+            part = jnp.broadcast_to(1.0 / total, (width, n_ex)).T
+            high, low = halves(users[b][...].astype(jnp.float32) * part)
+            scaled[b, :, :width] = high
+            scaled[b, :, width:] = low
+            if b:
+                continue
+            share[...] = part
+            pairs = users[0][...].astype(jnp.float32) * positive[...].astype(jnp.float32)
+            score = jnp.sum(jnp.sum(pairs, axis=0, keepdims=True), axis=1, keepdims=True)
+            loss = jnp.sum(jnp.log(total), axis=1, keepdims=True) - score / logit_divisor
+            rest = jnp.broadcast_to(loss, loss_row.shape)
+            lane = lax.broadcasted_iota(jnp.int32, loss_row.shape, 1)
+            row = jnp.zeros(loss_row.shape, jnp.float32)
+            for k in range(3):
+                term = rest.astype(jnp.bfloat16).astype(jnp.float32)
+                row = jnp.where(lane == k, term, row)
+                rest = rest - term
+            loss_row[...] = row
+
+    acc = jnp.zeros((item_cot.shape[0], 2 * width), jnp.float32)
+    for b, expo in enumerate(expos):
+        acc = acc + jnp.dot(expo[...], scaled[b], preferred_element_type=jnp.float32)
+    own_f = own[...].astype(jnp.float32)
+    own_f = jnp.where(step * own_f.shape[0] < n_ex, own_f, jnp.zeros_like(own_f))
+    item_cot[...] = (acc[:, :width] + acc[:, width:] - own_f) / logit_divisor
 
 
 def middle(expos, seen, users, items):
@@ -327,10 +320,11 @@
             jax.ShapeDtypeStruct((n_ex, width), jnp.float32),
             jax.ShapeDtypeStruct((1, width), jnp.float32),
         ],
+        scratch_shapes=[pltpu.VMEM((n_dp, n_ex, 2 * width), jnp.bfloat16)],
         cost_estimate=pl.CostEstimate(
-            flops=2 * n_dp * n_items * n_ex * width,
+            flops=4 * n_dp * n_items * n_ex * width,
             transcendentals=n_ex,
-            bytes_accessed=4 * n_dp * n_items * n_ex,
+            bytes_accessed=2 * n_dp * n_items * n_ex,
         ),
         name="middle",
     )(*expos, *seen, *users, users[0], items)
@@ -363,8 +357,8 @@
     cap = fetch_rows.shape[-1]
     n_ex = EXAMPLES_ON_CHIP
     asked = exchange(fetch_rows.reshape(n_all, cap))
-    fetched = id_table.at[asked.reshape(-1)].get(mode="promise_in_bounds")
-    slot_rows = exchange(fetched.reshape(n_all, cap, width)).reshape(-1, width)
+    fetched = id_table.at[asked].get(mode="promise_in_bounds")
+    slot_rows = exchange(fetched).reshape(-1, width)
     slot_index = lookup_slots[0]
     looked = slot_rows.at[slot_index].get(mode="promise_in_bounds")
 
@@ -381,35 +375,38 @@
             jnp.dot(item_bf, block.T, preferred_element_type=jnp.float32) / logit_divisor
         )
         parts.append(jnp.sum(expo, axis=0))
+        expos.append(expo.astype(jnp.bfloat16))
         pulls.append(
             lax.dot_general(
-                expo.astype(jnp.bfloat16),
-                item_bf,
-                (((0,), (0,)), ((), ())),
-                preferred_element_type=jnp.float32,
+                expos[-1], item_bf, (((0,), (0,)), ((), ())), preferred_element_type=jnp.float32
             )
         )
-        expos.append(expo)
     mine = jnp.stack(parts)
     seen = fetch([mine] * n_dp, "dp")
     returned = give([pulls[0]] + [p.astype(jnp.bfloat16) for p in pulls[1:]], "dp")
     item_cot, share, loss_row = middle(expos, seen, group_users, item_bf)
     positive = item_bf[:n_ex].astype(jnp.float32)
 
-    item_look, item_sums = tower_back(item_saved, item_cot)
+    item_look, item_sums = tower_back(looked, n_ex, item_saved, item_cot)
     pulled = sum(p.astype(jnp.float32) for p in returned)
     user_cot = (pulled * share - positive) / logit_divisor
     sent = exchange(
         tower_back(
-            user_saved, user_cot, (item_look, item_sums, lookup_slots, loss_row), n_all, cap
+            looked,
+            0,
+            user_saved,
+            user_cot,
+            (item_look, item_sums, lookup_slots, loss_row),
+            n_all,
+            cap,
         )
     )
     deep = sent.shape[1] - cap - 8
     chunk = jnp.sum(sent[:, : deep + 8].astype(jnp.float32), axis=0)
     mean_loss = jnp.sum(chunk[deep, :3]) / (n_all * n_ex)
     chunk = (chunk[:deep] / n_all).astype(jnp.bfloat16)
-    row = jnp.stack(fetch([chunk] * lax.axis_size("shard"), "shard"))
-    outs = spread(fetch([row] * n_dp, "dp"), (user_first, user_second, item_first, item_second))
+    whole = exchange(jnp.broadcast_to(chunk[None], (n_all, *chunk.shape))).reshape(-1, width)
+    outs = spread(whole, (user_first, user_second, item_first, item_second))
 
     new_table, new_state = update(id_table, ada_state, asked.reshape(n_all, 1, cap), sent)
     return (new_table, new_state, *outs, mean_loss)

time: 173 us -> 158 us (0.913)
  waiting for transfers between devices: 41 us -> 34.4 us
  starting transfers between devices: 20.6 us -> 16.3 us
  Pallas kernels: 34.1 us -> 31.9 us
    ppermute x16 -> x6, waiting for transfers between devices: 10.7 us -> 0.16 us  [fetch(): lax.ppermute(blocks[k], axis, [((i + k) % n, i) for i in range(n)])]
    ppermute x16 -> x6, starting transfers between devices: 14.8 us -> 6.94 us  [fetch(): lax.ppermute(blocks[k], axis, [((i + k) % n, i) for i in range(n)])]
    all_to_all x1 -> x2, waiting for transfers between devices: 30.2 us -> 34.2 us  [exchange(): return lax.all_to_all(x, AXES, split_axis=0, concat_axis=0, tiled=True)]
    all_to_all x1 -> x2, starting transfers between devices: 2.79 us -> 5.39 us  [exchange(): return lax.all_to_all(x, AXES, split_axis=0, concat_axis=0, tiled=True)]
    unnamed x68 -> x56, local copies, waits for them, and re-layouts: 3.18 us -> 3.53 us
  transfers between devices with their start and end apart: 20 -> 11, of which waited for: 7 -> 3; matrix products, arithmetic and copies ran while one was open for 3% -> 4% of each run, Pallas kernels for 14% -> 15%
where the time goes in v3:
time: 158 us; the launch traced here: 157 us
  blocking collectives  47.5 us (30%)
  waiting for transfers between devices  34.4 us (22%)
  Pallas kernels  31.9 us (20%)
  starting transfers between devices  16.3 us (10%)
  local copies, waits for them, and re-layouts  15 us (9%)
  matrix products  7.7 us (5%)
  between operations  2.95 us (2%)
  other arithmetic  1.91 us (1%)
    all_to_all x2, blocking collectives, exchange(): return lax.all_to_all(x, AXES, split_axis=0, concat_axis=0, tiled=True)  47.5 us
    all_to_all x2, waiting for transfers between devices, exchange(): return lax.all_to_all(x, AXES, split_axis=0, concat_axis=0, tiled=True)  34.2 us
    pallas_call x2, Pallas kernels, tower_back(): pl.pallas_call(functools.partial(back_kernel, last), grid=(n // rows,), i...  13.3 us
    pallas_call x1, Pallas kernels, update(): pl.pallas_call(functools.partial(update_kernel, skip), grid_spec=pltpu.Pr...  11 us
    gather x1, local copies, waits for them, and re-layouts, per_device(): fetched = id_table.at[asked].get(mode='promise_in_bounds')  7.28 us
    ppermute x6, starting transfers between devices, fetch(): lax.ppermute(blocks[k], axis, [((i + k) % n, i) for i in range(n)])  6.94 us
    pallas_call x1, Pallas kernels, middle(): pl.pallas_call(functools.partial(middle_kernel, n_dp, n_ex), grid=(n_item...  5.52 us
    all_to_all x2, starting transfers between devices, exchange(): return lax.all_to_all(x, AXES, split_axis=0, concat_axis=0, tiled=True)  5.39 us
  transfers between devices with their start and end apart: 11, of which 3 were waited for; matrix products, arithmetic and copies ran while one was open for 4% of the time, Pallas kernels for 15%

profile of v3, /device:TPU:0, one launch (start us, length us, event | category | flops | bytes accessed | tf_op | source)
XLA Modules:
  0.0 157.5 jit_solution(14344118789443396204)
XLA Ops:
  0.6 14.4 %all_to_all.27.rows_ref = s32[32,1,72]{2,1,0:T(1,128)S(1)} all-to-all(s32[32,1,72]{2,1,0:T(1,128)} %bitcast.40), channel_id=1, replica_groups=mesh['dp'=4,'shard'=8] {'dp','shard'}, dimensions={0} | all-to-all | bytes 18432 | tf_op jit(solution)/shard_map/all_to_all | solution.py:334
  15.2 7.3 %gather_fusion = f32[2304,128]{1,0:T(8,128)} fusion(f32[8192,128]{1,0:T(8,128)} %table.1, s32[3072]{0:T(1024)S(1)} %pad_clamp_fusion), kind=kCustom, calls=%fused_computation | custom fusion | bytes 2368512 | tf_op jit(solution)/shard_map/gather | solution.py:360
  22.5 2.8 %all-to-all-start.1 = ((f32[32,72,128]{2,1,0:T(8,128)}), f32[32,72,128]{2,1,0:T(8,128)S(1)}, u32[]{:S(2)}, u32[]{:S(2)}) async-start(f32[32,72,128]{2,1,0:T(8,128)} %bitcast.2), calls=%async_computation.1 | async-start | bytes 2359296 | tf_op jit(solution)/shard_map/all_to_all | solution.py:334
  25.3 30.2 %all-to-all-done.1 = f32[32,72,128]{2,1,0:T(8,128)S(1)} async-done(((f32[32,72,128]{2,1,0:T(8,128)}), f32[32,72,128]{2,1,0:T(8,128)S(1)}, u32[]{:S(2)}, u32[]{:S(2)}) %all-to-all-start.1) | async-done | bytes 1179680 | tf_op jit(solution)/shard_map/all_to_all | solution.py:334
  55.5 2.6 %gather_fusion.1 = f32[1536,128]{1,0:T(8,128)S(1)} fusion(f32[2304,128]{1,0:T(8,128)S(1)} %bitcast.36, s32[2048]{0:T(1024)S(1)} %pad_clamp_fusion.1), kind=kCustom, calls=%fused_computation.1 | custom fusion | bytes 1579008 | tf_op jit(solution)/shard_map/gather | solution.py:363
  59.3 0.8 multiply_reduce_fusion.1
  60.7 1.1 collective-permute-start.2
  61.8 2.3 %collective-permute-start = (bf16[512,128]{1,0:T(8,128)(2,1)S(1)}, bf16[512,128]{1,0:T(8,128)(2,1)S(1)}, u32[]{:S(2)}, u32[]{:S(2)}) collective-permute-start(bf16[512,128]{1,0:T(8,128)(2,1)S(1)} %divide_convert_fusion.1.refs_8_.refs_12_), channel_id=1, source_target_pairs={{8,0},{16,8},{24,16},{0,24},{9,1},{17,9},{25,17},{1,25},{10,2},{18... | collective-permute-start | bytes 393224 | tf_op jit(solution)/shard_map/ppermute | solution.py:340
  64.1 1.0 fusion.28.refs_1_
  65.1 1.5 multiply_reduce_fusion
  70.6 1.9 %collective-permute-start.6 = (f32[4,512]{1,0:T(4,128)S(1)}, f32[4,512]{1,0:T(4,128)S(1)}, u32[]{:S(2)}, u32[]{:S(2)}) collective-permute-start(f32[4,512]{1,0:T(4,128)S(1)} %pad_maximum_fusion.refs_4_), channel_id=1, source_target_pairs={{8,0},{16,8},{24,16},{0,24},{9,1},{17,9},{25,17},{1,25},{10,2},{18... | collective-permute-start | bytes 24584 | tf_op jit(solution)/shard_map/ppermute | solution.py:340
  72.5 1.1 collective-permute-start.7
  74.5 2.0 %collective-permute-start.1 = (bf16[512,128]{1,0:T(8,128)(2,1)S(1)}, bf16[512,128]{1,0:T(8,128)(2,1)S(1)}, u32[]{:S(2)}, u32[]{:S(2)}) collective-permute-start(bf16[512,128]{1,0:T(8,128)(2,1)S(1)} %convolution_convert_fusion.2), channel_id=1, source_target_pairs={{0,8},{8,16},{16,24},{24,0},{1,9},{9,17},{17,25},{25,1},{2,10},{10... | collective-permute-start | bytes 393224 | tf_op jit(solution)/shard_map/ppermute | solution.py:347
  77.0 1.2 collective-permute-start.3
  80.7 5.5 %middle.1 = (f32[1024,128]{1,0:T(8,128)}, f32[512,128]{1,0:T(8,128)}, f32[1,128]{1,0:T(1,128)}) custom-call(bf16[1024,512]{1,0:T(8,128)(2,1)} %copy-done.5, bf16[1024,512]{1,0:T(8,128)(2,1)} %copy-done.8, bf16[1024,512]{1,0:T(8,128)(2,1)} %copy-done.7, bf16[1024,512]{1,0:T(8,128)(2,1)} %copy-done.6, f32[4,512]{1,0:T(4,128)} %copy-done.22, ...), custom_call_target="tpu_custom_call" | custom-call | flops 1073741824 | bytes 4194304 | tf_op jit(solution)/shard_map/middle/pallas_call | solution.py:303
  86.2 6.8 %item_back.1 = (bf16[1024,128]{1,0:T(8,128)(2,1)}, bf16[1024,128]{1,0:T(8,128)(2,1)}) custom-call(f32[1536,128]{1,0:T(8,128)} %copy-done.3, f32[1024,512]{1,0:T(8,128)} %copy-done.10, f32[1024,128]{1,0:T(8,128)} %copy-done.11, f32[1024,128]{1,0:T(8,128)} %get-tuple-element.23.refs_3_, f32[128,512]{1,0:T(8,128)} %refs_4_.2, f32[512,128]{1,0:T(8,128)} %refs_5_.2), custom_call_target="tpu_custom_call" | custom-call | flops 1610612736 | bytes 4194304 | tf_op jit(solution)/shard_map/item_back/pallas_call | solution.py:142
  93.9 6.5 %user_back.1 = bf16[32,144,128]{2,1,0:T(8,128)(2,1)} custom-call(f32[1536,128]{1,0:T(8,128)} %copy-done.3, f32[512,512]{1,0:T(8,128)} %copy-done.4, f32[512,128]{1,0:T(8,128)} %copy-done.9, f32[512,128]{1,0:T(8,128)} %subtract_multiply_fusion.refs_3_, f32[128,512]{1,0:T(8,128)} %refs_4_.3, f32[512,128]{1,0:T(8,128)} %refs_5_.3, ...), custom_call_target="tpu_custom_call" | custom-call | flops 805306368 | bytes 2097152 | tf_op jit(solution)/shard_map/user_back/pallas_call | solution.py:142
  100.4 33.0 %all_to_all.28.grads = bf16[32,144,128]{2,1,0:T(8,128)(2,1)S(1)} all-to-all(bf16[32,144,128]{2,1,0:T(8,128)(2,1)} %user_back.1), channel_id=1, replica_groups=mesh['dp'=4,'shard'=8] {'dp','shard'}, dimensions={0} | all-to-all | bytes 2359296 | tf_op jit(solution)/shard_map/all_to_all | solution.py:334
  133.5 1.1 broadcast_in_dim.2
  134.7 2.6 %all-to-all-start.3 = ((bf16[32,64,128]{2,1,0:T(8,128)(2,1)}), bf16[32,64,128]{2,1,0:T(8,128)(2,1)S(1)}, u32[]{:S(2)}, u32[]{:S(2)}) async-start(bf16[32,64,128]{2,1,0:T(8,128)(2,1)} %broadcast_in_dim.2), calls=%async_computation.3 | async-start | bytes 1048576 | tf_op jit(solution)/shard_map/all_to_all | solution.py:334
  138.5 11.0 %update.1 = (f32[8192,128]{1,0:T(8,128)}, f32[64,128]{1,0:T(8,128)}) custom-call(s32[32,1,72]{2,1,0:T(1,128)} %copy-done.18, bf16[32,144,128]{2,1,0:T(8,128)(2,1)} %copy-done.2, f32[8192,128]{1,0:T(8,128)} %table.1, f32[64,128]{1,0:T(8,128)} %bitcast.39), custom_call_target="tpu_custom_call" | custom-call | flops 20971520 | bytes 8388608 | tf_op jit(solution)/shard_map/update/pallas_call | solution.py:201
  149.5 4.0 %all-to-all-done.3 = bf16[32,64,128]{2,1,0:T(8,128)(2,1)S(1)} async-done(((bf16[32,64,128]{2,1,0:T(8,128)(2,1)}), bf16[32,64,128]{2,1,0:T(8,128)(2,1)S(1)}, u32[]{:S(2)}, u32[]{:S(2)}) %all-to-all-start.3) | async-done | bytes 524320 | tf_op jit(solution)/shard_map/all_to_all | solution.py:334
  153.5 0.8 copy-done.12
  154.3 2.0 %spread.1 = (f32[128,512]{1,0:T(8,128)}, f32[512,128]{1,0:T(8,128)}, f32[128,512]{1,0:T(8,128)}, f32[512,128]{1,0:T(8,128)}) custom-call(bf16[2048,128]{1,0:T(8,128)(2,1)} %bitcast.37), custom_call_target="tpu_custom_call" | custom-call | flops 262144 | bytes 1572864 | tf_op jit(solution)/shard_map/spread/pallas_call | solution.py:241
  (93 shorter events, 10.9 us)
Async XLA Ops:
  15.1 7.4 %copy-start.18 = (s32[32,1,72]{2,1,0:T(1,128)}, s32[32,1,72]{2,1,0:T(1,128)S(1)}, u32[]{:S(2)}) copy-start(s32[32,1,72]{2,1,0:T(1,128)S(1)} %all_to_all.27.rows_ref) | copy-start | bytes 27652
  22.5 33.1 %all-to-all-start.1 = ((f32[32,72,128]{2,1,0:T(8,128)}), f32[32,72,128]{2,1,0:T(8,128)S(1)}, u32[]{:S(2)}, u32[]{:S(2)}) async-start(f32[32,72,128]{2,1,0:T(8,128)} %bitcast.2), calls=%async_computation.1 | async-start | bytes 2359296 | tf_op jit(solution)/shard_map/all_to_all | solution.py:334
  60.4 6.2 %copy-start.9 = (f32[512,128]{1,0:T(8,128)}, f32[512,128]{1,0:T(8,128)S(1)}, u32[]{:S(2)}) copy-start(f32[512,128]{1,0:T(8,128)S(1)} %copy.22.refs_2_) | copy-start | bytes 786436
  60.6 7.3 %copy-start.13 = (bf16[512,128]{1,0:T(8,128)(2,1)}, bf16[512,128]{1,0:T(8,128)(2,1)S(1)}, u32[]{:S(2)}) copy-start(bf16[512,128]{1,0:T(8,128)(2,1)S(1)} %divide_convert_fusion.1.refs_8_.refs_12_) | copy-start | bytes 393220
  60.6 8.3 %collective-permute-start.4 = (bf16[512,128]{1,0:T(8,128)(2,1)S(1)}, bf16[512,128]{1,0:T(8,128)(2,1)S(1)}, u32[]{:S(2)}, u32[]{:S(2)}) collective-permute-start(bf16[512,128]{1,0:T(8,128)(2,1)S(1)} %divide_convert_fusion.1.refs_8_.refs_12_), channel_id=1, source_target_pairs={{24,0},{0,8},{8,16},{16,24},{25,1},{1,9},{9,17},{17,25},{26,2},{2,... | collective-permute-start | bytes 393224 | tf_op jit(solution)/shard_map/ppermute | solution.py:340
  60.7 8.8 %collective-permute-start.2 = (bf16[512,128]{1,0:T(8,128)(2,1)S(1)}, bf16[512,128]{1,0:T(8,128)(2,1)S(1)}, u32[]{:S(2)}, u32[]{:S(2)}) collective-permute-start(bf16[512,128]{1,0:T(8,128)(2,1)S(1)} %divide_convert_fusion.1.refs_8_.refs_12_), channel_id=1, source_target_pairs={{16,0},{24,8},{0,16},{8,24},{17,1},{25,9},{1,17},{9,25},{18,2},{26... | collective-permute-start | bytes 393224 | tf_op jit(solution)/shard_map/ppermute | solution.py:340
  61.8 8.3 %collective-permute-start = (bf16[512,128]{1,0:T(8,128)(2,1)S(1)}, bf16[512,128]{1,0:T(8,128)(2,1)S(1)}, u32[]{:S(2)}, u32[]{:S(2)}) collective-permute-start(bf16[512,128]{1,0:T(8,128)(2,1)S(1)} %divide_convert_fusion.1.refs_8_.refs_12_), channel_id=1, source_target_pairs={{8,0},{16,8},{24,16},{0,24},{9,1},{17,9},{25,17},{1,25},{10,2},{18... | collective-permute-start | bytes 393224 | tf_op jit(solution)/shard_map/ppermute | solution.py:340
  67.9 10.4 %copy-start = (bf16[1024,128]{1,0:T(8,128)(2,1)}, bf16[1024,128]{1,0:T(8,128)(2,1)S(1)}, u32[]{:S(2)}) copy-start(bf16[1024,128]{1,0:T(8,128)(2,1)S(1)} %divide_convert_fusion.refs_13_) | copy-start | bytes 786436
  69.4 8.9 %copy-start.6 = (bf16[1024,512]{1,0:T(8,128)(2,1)}, bf16[1024,512]{1,0:T(8,128)(2,1)S(1)}, u32[]{:S(2)}) copy-start(bf16[1024,512]{1,0:T(8,128)(2,1)S(1)} %get-tuple-element.40.refs_3_) | copy-start | bytes 3145732
  69.5 5.0 %copy-start.20 = (bf16[512,128]{1,0:T(8,128)(2,1)}, bf16[512,128]{1,0:T(8,128)(2,1)S(1)}, u32[]{:S(2)}) copy-start(bf16[512,128]{1,0:T(8,128)(2,1)S(1)} %collective-permute-done.2.refs_10_) | copy-start | bytes 393220
  70.0 7.0 %copy-start.7 = (bf16[1024,512]{1,0:T(8,128)(2,1)}, bf16[1024,512]{1,0:T(8,128)(2,1)S(1)}, u32[]{:S(2)}) copy-start(bf16[1024,512]{1,0:T(8,128)(2,1)S(1)} %get-tuple-element.38.refs_2_) | copy-start | bytes 3145732
  70.0 7.0 %copy-start.21 = (bf16[512,128]{1,0:T(8,128)(2,1)}, bf16[512,128]{1,0:T(8,128)(2,1)S(1)}, u32[]{:S(2)}) copy-start(bf16[512,128]{1,0:T(8,128)(2,1)S(1)} %collective-permute-done.refs_9_) | copy-start | bytes 393220
  70.5 8.2 %copy-start.8 = (bf16[1024,512]{1,0:T(8,128)(2,1)}, bf16[1024,512]{1,0:T(8,128)(2,1)S(1)}, u32[]{:S(2)}) copy-start(bf16[1024,512]{1,0:T(8,128)(2,1)S(1)} %get-tuple-element.36.refs_1_) | copy-start | bytes 3145732
  70.6 8.1 %copy-start.22 = (f32[4,512]{1,0:T(4,128)}, f32[4,512]{1,0:T(4,128)S(1)}, u32[]{:S(2)}) copy-start(f32[4,512]{1,0:T(4,128)S(1)} %pad_maximum_fusion.refs_4_) | copy-start | bytes 24580
  70.6 8.1 %collective-permute-start.6 = (f32[4,512]{1,0:T(4,128)S(1)}, f32[4,512]{1,0:T(4,128)S(1)}, u32[]{:S(2)}, u32[]{:S(2)}) collective-permute-start(f32[4,512]{1,0:T(4,128)S(1)} %pad_maximum_fusion.refs_4_), channel_id=1, source_target_pairs={{8,0},{16,8},{24,16},{0,24},{9,1},{17,9},{25,17},{1,25},{10,2},{18... | collective-permute-start | bytes 24584 | tf_op jit(solution)/shard_map/ppermute | solution.py:340
  72.5 7.0 %collective-permute-start.7 = (f32[4,512]{1,0:T(4,128)S(1)}, f32[4,512]{1,0:T(4,128)S(1)}, u32[]{:S(2)}, u32[]{:S(2)}) collective-permute-start(f32[4,512]{1,0:T(4,128)S(1)} %pad_maximum_fusion.refs_4_), channel_id=1, source_target_pairs={{16,0},{24,8},{0,16},{8,24},{17,1},{25,9},{1,17},{9,25},{18,2},{26... | collective-permute-start | bytes 24584 | tf_op jit(solution)/shard_map/ppermute | solution.py:340
  73.6 5.9 %collective-permute-start.8 = (f32[4,512]{1,0:T(4,128)S(1)}, f32[4,512]{1,0:T(4,128)S(1)}, u32[]{:S(2)}, u32[]{:S(2)}) collective-permute-start(f32[4,512]{1,0:T(4,128)S(1)} %pad_maximum_fusion.refs_4_), channel_id=1, source_target_pairs={{24,0},{0,8},{8,16},{16,24},{25,1},{1,9},{9,17},{17,25},{26,2},{2,... | collective-permute-start | bytes 24584 | tf_op jit(solution)/shard_map/ppermute | solution.py:340
  74.5 18.5 %collective-permute-start.1 = (bf16[512,128]{1,0:T(8,128)(2,1)S(1)}, bf16[512,128]{1,0:T(8,128)(2,1)S(1)}, u32[]{:S(2)}, u32[]{:S(2)}) collective-permute-start(bf16[512,128]{1,0:T(8,128)(2,1)S(1)} %convolution_convert_fusion.2), channel_id=1, source_target_pairs={{0,8},{8,16},{16,24},{24,0},{1,9},{9,17},{17,25},{25,1},{2,10},{10... | collective-permute-start | bytes 393224 | tf_op jit(solution)/shard_map/ppermute | solution.py:347
  77.0 16.0 %collective-permute-start.3 = (bf16[512,128]{1,0:T(8,128)(2,1)S(1)}, bf16[512,128]{1,0:T(8,128)(2,1)S(1)}, u32[]{:S(2)}, u32[]{:S(2)}) collective-permute-start(bf16[512,128]{1,0:T(8,128)(2,1)S(1)} %convolution_convert_fusion.1), channel_id=1, source_target_pairs={{0,16},{8,24},{16,0},{24,8},{1,17},{9,25},{17,1},{25,9},{2,18},{10... | collective-permute-start | bytes 393224 | tf_op jit(solution)/shard_map/ppermute | solution.py:347
  78.7 14.3 %collective-permute-start.5 = (bf16[512,128]{1,0:T(8,128)(2,1)S(1)}, bf16[512,128]{1,0:T(8,128)(2,1)S(1)}, u32[]{:S(2)}, u32[]{:S(2)}) collective-permute-start(bf16[512,128]{1,0:T(8,128)(2,1)S(1)} %convolution_convert_fusion), channel_id=1, source_target_pairs={{0,24},{8,0},{16,8},{24,16},{1,25},{9,1},{17,9},{25,17},{2,26},{10... | collective-permute-start | bytes 393224 | tf_op jit(solution)/shard_map/ppermute | solution.py:347
  86.2 6.9 %copy-start.1 = (bf16[1024,128]{1,0:T(8,128)(2,1)S(1)}, bf16[1024,128]{1,0:T(8,128)(2,1)}, u32[]{:S(2)}) copy-start(bf16[1024,128]{1,0:T(8,128)(2,1)} %copy-done) | copy-start | bytes 786436
  86.2 6.9 %copy-start.16 = (f32[512,128]{1,0:T(8,128)S(1)}, f32[512,128]{1,0:T(8,128)}, u32[]{:S(2)}) copy-start(f32[512,128]{1,0:T(8,128)} %get-tuple-element.22) | copy-start | bytes 786436
  133.4 5.1 %copy-start.2 = (bf16[32,144,128]{2,1,0:T(8,128)(2,1)}, bf16[32,144,128]{2,1,0:T(8,128)(2,1)S(1)}, u32[]{:S(2)}) copy-start(bf16[32,144,128]{2,1,0:T(8,128)(2,1)S(1)} %all_to_all.28.grads) | copy-start | bytes 3538948
  134.7 18.8 %all-to-all-start.3 = ((bf16[32,64,128]{2,1,0:T(8,128)(2,1)}), bf16[32,64,128]{2,1,0:T(8,128)(2,1)S(1)}, u32[]{:S(2)}, u32[]{:S(2)}) async-start(bf16[32,64,128]{2,1,0:T(8,128)(2,1)} %broadcast_in_dim.2), calls=%async_computation.3 | async-start | bytes 1048576 | tf_op jit(solution)/shard_map/all_to_all | solution.py:334
  (15 other events, 27.6 us)

commit v4 on v3

--- a/solution.py
+++ b/solution.py
@@ -45,10 +45,16 @@
     return one(ah, bh) + one(al, bh) + one(ah, bl)
 
 
-def back_kernel(last, *refs):
-    looked, hidden, out, cot, first_w, second_w = refs[:6]
+def narrow_dot(a, b, dims):
+    a, b = a.astype(jnp.bfloat16), b.astype(jnp.bfloat16)
+    return lax.dot_general(a, b, (dims, ((), ())), preferred_element_type=jnp.float32)
+
+
+def back_kernel(last, n_cots, *refs):
+    cots, refs = refs[:n_cots], refs[n_cots:]
+    looked, hidden, out, first_w, second_w = refs[:5]
     first_g, second_g = refs[-2:]
-    look_g = refs[-3] if last else refs[6]
+    look_g = refs[-3] if last else refs[5]
     step = pl.program_id(0)
 
     @pl.when(step == 0)
@@ -56,7 +62,13 @@
         first_g[...] = jnp.zeros_like(first_g)
         second_g[...] = jnp.zeros_like(second_g)
 
-    z, g, h = out[...], cot[...], hidden[...]
+    z, h = out[...], hidden[...]
+    if last:
+        *pulled, share, positive = cots
+        g = sum(p[...].astype(jnp.float32) for p in pulled) * share[...]
+        g = (g - positive[...].astype(jnp.float32)) / logit_divisor
+    else:
+        g = cots[0][...]
     rows, width = z.shape
     inverse = 1.0 / jnp.sqrt(jnp.sum(z * z, axis=1, keepdims=True) + 1e-06)
     vec = z * inverse
@@ -66,13 +78,13 @@
     slope = gate + active * (1.0 - gate)
     hidden_cot = wide_dot(halves(out_cot), halves(second_w[...]), ((1,), (1,))) * slope
     both = halves(hidden_cot)
-    mine = wide_dot(both, halves(first_w[...]), ((1,), (1,))).astype(look_g.dtype)
+    mine = narrow_dot(hidden_cot, first_w[...], ((1,), (1,))).astype(look_g.dtype)
     if last:
         look_g[pl.ds(pl.multiple_of(step * rows, rows), rows), :] = mine
     else:
         look_g[...] = mine
     first_g[...] += wide_dot(halves(looked[...].T), both, ((1,), (0,)))
-    second_g[...] += wide_dot(halves(out_cot.T), halves(active), ((1,), (0,)))
+    second_g[...] += narrow_dot(out_cot.T, active, ((1,), (0,)))
 
     @pl.when(step == pl.num_programs(0) - 1)
     def _():
@@ -81,9 +93,9 @@
         flat = [f.astype(jnp.bfloat16) for f in flat]
         if not last:
             for k, f in enumerate(flat):
-                refs[7][k * width : (k + 1) * width, :] = f
+                refs[6][k * width : (k + 1) * width, :] = f
             return
-        item_look, item_sums, lookups, loss_row, sent = refs[6:11]
+        item_look, item_sums, lookups, loss_row, sent = refs[5:10]
         n_all = sent.shape[0]
         deep = 2 * len(flat) * width // n_all
         cap = sent.shape[1] - deep - 8
@@ -114,7 +126,7 @@
                 sent[k + j, deep + 8 :, :] = total[j * cap : (j + 1) * cap].astype(sent.dtype)
 
 
-def tower_back(looked, start, saved, cot, rest=(), n_all=0, cap=0):
+def tower_back(looked, start, saved, cots, rest=(), n_all=0, cap=0):
     hidden, out, first_w, second_w = saved
     n, width = out.shape
     inner = hidden.shape[1]
@@ -140,10 +152,11 @@
         ]
         scratch = []
     return pl.pallas_call(
-        functools.partial(back_kernel, last),
+        functools.partial(back_kernel, last, len(cots)),
         grid=(n // rows,),
-        in_specs=[pl.BlockSpec((rows, width), lambda i: (i + start // rows, 0))]
-        + [by_rows(inner), by_rows(width), by_rows(width)]
+        in_specs=[by_rows(width)] * len(cots)
+        + [pl.BlockSpec((rows, width), lambda i: (i + start // rows, 0))]
+        + [by_rows(inner), by_rows(width)]
         + [fixed(x.shape) for x in (first_w, second_w, *rest)],
         out_specs=out_specs,
         out_shape=out_shape,
@@ -153,8 +166,9 @@
             transcendentals=n * inner,
             bytes_accessed=4 * n * (inner + 4 * width),
         ),
+        compiler_params=pltpu.CompilerParams(vmem_limit_bytes=32 << 20),
         name="user_back" if last else "item_back",
-    )(looked, hidden, out, cot, first_w, second_w, *rest)
+    )(*cots, looked, hidden, out, first_w, second_w, *rest)
 
 
 def update_kernel(skip, rows_ref, grads, table, state, new_table, new_state, *totals):
@@ -221,6 +235,7 @@
         cost_estimate=pl.CostEstimate(
             flops=20 * n * width, transcendentals=n, bytes_accessed=8 * n * width
         ),
+        compiler_params=pltpu.CompilerParams(vmem_limit_bytes=40 << 20),
         name="update",
     )(rows_of, grads, table, state)
     return new_table, new_state.reshape(-1)
@@ -326,6 +341,7 @@
             transcendentals=n_ex,
             bytes_accessed=2 * n_dp * n_items * n_ex,
         ),
+        compiler_params=pltpu.CompilerParams(vmem_limit_bytes=32 << 20),
         name="middle",
     )(*expos, *seen, *users, users[0], items)
 
@@ -385,17 +401,14 @@
     seen = fetch([mine] * n_dp, "dp")
     returned = give([pulls[0]] + [p.astype(jnp.bfloat16) for p in pulls[1:]], "dp")
     item_cot, share, loss_row = middle(expos, seen, group_users, item_bf)
-    positive = item_bf[:n_ex].astype(jnp.float32)
-
-    item_look, item_sums = tower_back(looked, n_ex, item_saved, item_cot)
-    pulled = sum(p.astype(jnp.float32) for p in returned)
-    user_cot = (pulled * share - positive) / logit_divisor
+
+    item_look, item_sums = tower_back(looked, n_ex, item_saved, (item_cot,))
     sent = exchange(
         tower_back(
             looked,
             0,
             user_saved,
-            user_cot,
+            (*returned, share, item_bf),
             (item_look, item_sums, lookup_slots, loss_row),
             n_all,
             cap,

time: 158 us -> 152 us (0.962)
  Pallas kernels: 31.9 us -> 21 us
  matrix products: 7.7 us -> 12.8 us
    pallas_call x2, Pallas kernels: 13.3 us -> 6.7 us  [tower_back(): pl.pallas_call(functools.partial(back_kernel, last, len(cots)), grid=(n /...]
    dot_general x4, matrix products: 1.95 us -> 4.66 us  [per_device(): jnp.dot(item_bf, block.T, preferred_element_type=jnp.float32)]
    dot_general x4, matrix products: 3.84 us -> 6.26 us  [product(): lax.dot_general(a, b, (dims, ((), ())), precision=fine, preferred_element...]
    pallas_call x1, Pallas kernels: 5.52 us -> 3.32 us  [middle(): pl.pallas_call(functools.partial(middle_kernel, n_dp, n_ex), grid=(n_item...]
    pallas_call x1, Pallas kernels: 11 us -> 8.98 us  [update(): pl.pallas_call(functools.partial(update_kernel, skip), grid_spec=pltpu.Pr...]
    unnamed x56 -> x24, local copies, waits for them, and re-layouts: 3.53 us -> 3.04 us
  transfers between devices with their start and end apart: 11 -> 11, of which waited for: 3 -> 2; matrix products, arithmetic and copies ran while one was open for 4% -> 8% of each run, Pallas kernels for 15% -> 10%
where the time goes in v4:
time: 152 us
  blocking collectives  47.7 us (31%)
  waiting for transfers between devices  34 us (22%)
  Pallas kernels  21 us (14%)
  local copies, waits for them, and re-layouts  16.1 us (11%)
  starting transfers between devices  15.4 us (10%)
  matrix products  12.8 us (8%)
  between operations  2.8 us (2%)
  other arithmetic  1.82 us (1%)
    all_to_all x2, blocking collectives, exchange(): return lax.all_to_all(x, AXES, split_axis=0, concat_axis=0, tiled=True)  47.7 us
    all_to_all x2, waiting for transfers between devices, exchange(): return lax.all_to_all(x, AXES, split_axis=0, concat_axis=0, tiled=True)  34 us
    pallas_call x1, Pallas kernels, update(): pl.pallas_call(functools.partial(update_kernel, skip), grid_spec=pltpu.Pr...  8.98 us
    gather x1, local copies, waits for them, and re-layouts, per_device(): fetched = id_table.at[asked].get(mode='promise_in_bounds')  7.28 us
    ppermute x6, starting transfers between devices, fetch(): lax.ppermute(blocks[k], axis, [((i + k) % n, i) for i in range(n)])  7.07 us
    pallas_call x2, Pallas kernels, tower_back(): pl.pallas_call(functools.partial(back_kernel, last, len(cots)), grid=(n /...  6.7 us
    dot_general x4, matrix products, product(): lax.dot_general(a, b, (dims, ((), ())), precision=fine, preferred_element...  6.26 us
    all_to_all x2, starting transfers between devices, exchange(): return lax.all_to_all(x, AXES, split_axis=0, concat_axis=0, tiled=True)  5.39 us
  transfers between devices with their start and end apart: 11, of which 2 were waited for; matrix products, arithmetic and copies ran while one was open for 8% of the time, Pallas kernels for 10%

profile of v4, /device:TPU:0, one launch (start us, length us, event | category | flops | bytes accessed | tf_op | source)
XLA Modules:
  0.0 151.7 jit_solution(10859472893335805328)
XLA Ops:
  0.6 14.4 %all_to_all.27.rows_ref = s32[32,1,72]{2,1,0:T(1,128)S(1)} all-to-all(s32[32,1,72]{2,1,0:T(1,128)} %bitcast.40), channel_id=1, replica_groups=mesh['dp'=4,'shard'=8] {'dp','shard'}, dimensions={0} | all-to-all | bytes 18432 | tf_op jit(solution)/shard_map/all_to_all | solution.py:350
  15.2 7.3 %gather_fusion = f32[2304,128]{1,0:T(8,128)} fusion(f32[8192,128]{1,0:T(8,128)} %table.1, s32[3072]{0:T(1024)S(1)} %pad_clamp_fusion), kind=kCustom, calls=%fused_computation | custom fusion | bytes 2368512 | tf_op jit(solution)/shard_map/gather | solution.py:376
  22.5 2.8 %all-to-all-start.1 = ((f32[32,72,128]{2,1,0:T(8,128)}), f32[32,72,128]{2,1,0:T(8,128)S(1)}, u32[]{:S(2)}, u32[]{:S(2)}) async-start(f32[32,72,128]{2,1,0:T(8,128)} %bitcast.2), calls=%async_computation.1 | async-start | bytes 2359296 | tf_op jit(solution)/shard_map/all_to_all | solution.py:350
  25.3 30.2 %all-to-all-done.1 = f32[32,72,128]{2,1,0:T(8,128)S(1)} async-done(((f32[32,72,128]{2,1,0:T(8,128)}), f32[32,72,128]{2,1,0:T(8,128)S(1)}, u32[]{:S(2)}, u32[]{:S(2)}) %all-to-all-start.1) | async-done | bytes 1179680 | tf_op jit(solution)/shard_map/all_to_all | solution.py:350
  55.5 2.6 %gather_fusion.1 = f32[1536,128]{1,0:T(8,128)S(1)} fusion(f32[2304,128]{1,0:T(8,128)S(1)} %bitcast.38, s32[2048]{0:T(1024)S(1)} %pad_clamp_fusion.1), kind=kCustom, calls=%fused_computation.1 | custom fusion | bytes 1579008 | tf_op jit(solution)/shard_map/gather | solution.py:379
  61.9 2.3 %collective-permute-start = (bf16[512,128]{1,0:T(8,128)(2,1)S(1)}, bf16[512,128]{1,0:T(8,128)(2,1)}, u32[]{:S(2)}, u32[]{:S(2)}) collective-permute-start(bf16[512,128]{1,0:T(8,128)(2,1)S(1)} %divide_convert_fusion.1.refs_8_.refs_12_), channel_id=1, source_target_pairs={{8,0},{16,8},{24,16},{0,24},{9,1},{17,9},{25,17},{1,25},{10,2},{18... | collective-permute-start | bytes 393224 | tf_op jit(solution)/shard_map/ppermute | solution.py:356
  64.2 2.0 %fusion.28.refs_2_ = f32[1024,512]{1,0:T(8,128)S(1)} fusion(f32[1024,128]{1,0:T(8,128)} %slice.24, f32[128,512]{1,0:T(8,128)S(1)} %copy-done.5), kind=kOutput, calls=%fused_computation.51 | convolution fusion | flops 402653184 | bytes 2883584 | tf_op jit(solution)/shard_map/dot_general | solution.py:21
  66.3 2.9 %multiply_reduce_fusion = (f32[1024]{0:T(1024)}, f32[1024,128]{0,1:T(8,128)}) fusion(f32[512,128]{1,0:T(8,128)S(1)} %copy-done.9, f32[1024,512]{1,0:T(8,128)S(1)} %fusion.28.refs_2_), kind=kOutput, calls=%fused_computation.32 | convolution fusion | flops 405011456 | bytes 2887680 | tf_op jit(solution)/shard_map/dot_general | solution.py:21
  69.1 1.2 copy.20.refs_3_
  72.3 1.4 fusion.12
  73.7 1.4 fusion.10
  75.1 1.4 fusion.8
  76.6 1.5 collective-permute-start.7
  78.1 1.9 %collective-permute-start.8 = (f32[4,512]{1,0:T(4,128)S(1)}, f32[4,512]{1,0:T(4,128)S(1)}, u32[]{:S(2)}, u32[]{:S(2)}) collective-permute-start(f32[4,512]{1,0:T(4,128)S(1)} %pad_maximum_fusion.refs_4_), channel_id=1, source_target_pairs={{24,0},{0,8},{8,16},{16,24},{25,1},{1,9},{9,17},{17,25},{26,2},{2,... | collective-permute-start | bytes 24584 | tf_op jit(solution)/shard_map/ppermute | solution.py:356
  83.2 1.3 collective-permute-start.1
  84.5 3.3 %middle.1 = (f32[1024,128]{1,0:T(8,128)S(1)}, f32[512,128]{1,0:T(8,128)S(1)}, f32[1,128]{1,0:T(1,128)S(1)}) custom-call(bf16[1024,512]{1,0:T(8,128)(2,1)S(1)} %get-tuple-element.34.refs_0_, bf16[1024,512]{1,0:T(8,128)(2,1)S(1)} %get-tuple-element.36.refs_1_, bf16[1024,512]{1,0:T(8,128)(2,1)S(1)} %get-tuple-element.38.refs_2_, ...), custom_call_target="tpu_custom_call" | custom-call | flops 1073741824 | bytes 4194304 | tf_op jit(solution)/shard_map/middle/pallas_call | solution.py:318
  87.8 3.3 %item_back.1 = (bf16[1024,128]{1,0:T(8,128)(2,1)S(1)}, bf16[1024,128]{1,0:T(8,128)(2,1)S(1)}) custom-call(f32[1024,128]{1,0:T(8,128)S(1)} %get-tuple-element.23.refs_0_, f32[1536,128]{1,0:T(8,128)S(1)} %gather_fusion.1, f32[1024,512]{1,0:T(8,128)S(1)} %copy-done.2, f32[1024,128]{1,0:T(8,128)S(1)} %copy.20.refs_3_, f32[128,512]{1,0:T(8,128)S(1)} %copy-done.5, ...), custom_call_target="tpu_custom_call" | custom-call | flops 1610612736 | bytes 4194304 | tf_op jit(solution)/shard_map/item_back/pallas_call | solution.py:154
  91.2 3.4 %user_back.1 = bf16[32,144,128]{2,1,0:T(8,128)(2,1)S(1)} custom-call(f32[512,128]{1,0:T(8,128)S(1)} %fusion.29.refs_0_, bf16[512,128]{1,0:T(8,128)(2,1)S(1)} %collective-permute-done.1.refs_1_, bf16[512,128]{1,0:T(8,128)(2,1)S(1)} %collective-permute-done.3.refs_2_, bf16[512,128]{1,0:T(8,128)(2,1)S(1)} %collective-permute-done.5.refs_3_, ...), custom_call_target="tpu_custom_call" | custom-call | flops 805306368 | bytes 2097152 | tf_op jit(solution)/shard_map/user_back/pallas_call | solution.py:154
  94.6 33.3 %all_to_all.28.grads = bf16[32,144,128]{2,1,0:T(8,128)(2,1)S(1)} all-to-all(bf16[32,144,128]{2,1,0:T(8,128)(2,1)S(1)} %user_back.1), channel_id=1, replica_groups=mesh['dp'=4,'shard'=8] {'dp','shard'}, dimensions={0} | all-to-all | bytes 2359296 | tf_op jit(solution)/shard_map/all_to_all | solution.py:350
  128.9 2.6 %all-to-all-start.3 = ((bf16[32,64,128]{2,1,0:T(8,128)(2,1)}), bf16[32,64,128]{2,1,0:T(8,128)(2,1)S(1)}, u32[]{:S(2)}, u32[]{:S(2)}) async-start(bf16[32,64,128]{2,1,0:T(8,128)(2,1)} %broadcast_in_dim.2), calls=%async_computation.3 | async-start | bytes 1048576 | tf_op jit(solution)/shard_map/all_to_all | solution.py:350
  132.8 2.2 %copy-done = f32[8192,128]{1,0:T(8,128)S(1)} copy-done((f32[8192,128]{1,0:T(8,128)S(1)}, f32[8192,128]{1,0:T(8,128)}, u32[]{:S(2)}) %copy-start) | copy-done | bytes 4194328
  135.0 9.0 %update.1 = (f32[8192,128]{1,0:T(8,128)}, f32[64,128]{1,0:T(8,128)}) custom-call(s32[32,1,72]{2,1,0:T(1,128)S(1)} %all_to_all.27.rows_ref, bf16[32,144,128]{2,1,0:T(8,128)(2,1)S(1)} %all_to_all.28.grads, f32[8192,128]{1,0:T(8,128)S(1)} %copy-done, f32[64,128]{1,0:T(8,128)S(1)} %bitcast.37), custom_call_target="tpu_custom_call" | custom-call | flops 20971520 | bytes 8388608 | tf_op jit(solution)/shard_map/update/pallas_call | solution.py:215
  144.0 3.8 %all-to-all-done.3 = bf16[32,64,128]{2,1,0:T(8,128)(2,1)S(1)} async-done(((bf16[32,64,128]{2,1,0:T(8,128)(2,1)}), bf16[32,64,128]{2,1,0:T(8,128)(2,1)S(1)}, u32[]{:S(2)}, u32[]{:S(2)}) %all-to-all-start.3) | async-done | bytes 524320 | tf_op jit(solution)/shard_map/all_to_all | solution.py:350
  148.6 2.0 %spread.1 = (f32[128,512]{1,0:T(8,128)}, f32[512,128]{1,0:T(8,128)}, f32[128,512]{1,0:T(8,128)}, f32[512,128]{1,0:T(8,128)}) custom-call(bf16[2048,128]{1,0:T(8,128)(2,1)} %bitcast.39), custom_call_target="tpu_custom_call" | custom-call | flops 262144 | bytes 1572864 | tf_op jit(solution)/shard_map/spread/pallas_call | solution.py:256
  (60 shorter events, 11.4 us)
Async XLA Ops:
  22.5 2.8 %copy-start.7 = (s32[1,1536]{1,0:T(1,128)S(1)}, s32[1,1536]{1,0:T(1,128)}, u32[]{:S(2)}) copy-start(s32[1,1536]{1,0:T(1,128)} %refs_13_.1) | copy-start | bytes 18436
  22.5 33.1 %all-to-all-start.1 = ((f32[32,72,128]{2,1,0:T(8,128)}), f32[32,72,128]{2,1,0:T(8,128)S(1)}, u32[]{:S(2)}, u32[]{:S(2)}) async-start(f32[32,72,128]{2,1,0:T(8,128)} %bitcast.2), calls=%async_computation.1 | async-start | bytes 2359296 | tf_op jit(solution)/shard_map/all_to_all | solution.py:350
  55.5 3.4 %copy-start.3 = (f32[128,512]{1,0:T(8,128)S(1)}, f32[128,512]{1,0:T(8,128)}, u32[]{:S(2)}) copy-start(f32[128,512]{1,0:T(8,128)} %refs_9_.1) | copy-start | bytes 786436
  58.1 1.4 copy-start.4
  59.6 4.7 %copy-start.5 = (f32[128,512]{1,0:T(8,128)S(1)}, f32[128,512]{1,0:T(8,128)}, u32[]{:S(2)}) copy-start(f32[128,512]{1,0:T(8,128)} %refs_4_.1) | copy-start | bytes 786436
  60.4 5.8 %copy-start.9 = (f32[512,128]{1,0:T(8,128)S(1)}, f32[512,128]{1,0:T(8,128)}, u32[]{:S(2)}) copy-start(f32[512,128]{1,0:T(8,128)} %refs_5_.1) | copy-start | bytes 786436
  60.7 11.6 %collective-permute-start.4 = (bf16[512,128]{1,0:T(8,128)(2,1)S(1)}, bf16[512,128]{1,0:T(8,128)(2,1)}, u32[]{:S(2)}, u32[]{:S(2)}) collective-permute-start(bf16[512,128]{1,0:T(8,128)(2,1)S(1)} %divide_convert_fusion.1.refs_8_.refs_12_), channel_id=1, source_target_pairs={{24,0},{0,8},{8,16},{16,24},{25,1},{1,9},{9,17},{17,25},{26,2},{2,... | collective-permute-start | bytes 393224 | tf_op jit(solution)/shard_map/ppermute | solution.py:356
  60.8 12.9 %collective-permute-start.2 = (bf16[512,128]{1,0:T(8,128)(2,1)S(1)}, bf16[512,128]{1,0:T(8,128)(2,1)}, u32[]{:S(2)}, u32[]{:S(2)}) collective-permute-start(bf16[512,128]{1,0:T(8,128)(2,1)S(1)} %divide_convert_fusion.1.refs_8_.refs_12_), channel_id=1, source_target_pairs={{16,0},{24,8},{0,16},{8,24},{17,1},{25,9},{1,17},{9,25},{18,2},{26... | collective-permute-start | bytes 393224 | tf_op jit(solution)/shard_map/ppermute | solution.py:356
  61.9 13.2 %collective-permute-start = (bf16[512,128]{1,0:T(8,128)(2,1)S(1)}, bf16[512,128]{1,0:T(8,128)(2,1)}, u32[]{:S(2)}, u32[]{:S(2)}) collective-permute-start(bf16[512,128]{1,0:T(8,128)(2,1)S(1)} %divide_convert_fusion.1.refs_8_.refs_12_), channel_id=1, source_target_pairs={{8,0},{16,8},{24,16},{0,24},{9,1},{17,9},{25,17},{1,25},{10,2},{18... | collective-permute-start | bytes 393224 | tf_op jit(solution)/shard_map/ppermute | solution.py:356
  66.2 2.9 %copy-start.1 = (f32[1024,512]{1,0:T(8,128)}, f32[1024,512]{1,0:T(8,128)S(1)}, u32[]{:S(2)}) copy-start(f32[1024,512]{1,0:T(8,128)S(1)} %fusion.28.refs_2_) | copy-start | bytes 6291460
  76.5 6.7 %collective-permute-start.6 = (f32[4,512]{1,0:T(4,128)S(1)}, f32[4,512]{1,0:T(4,128)S(1)}, u32[]{:S(2)}, u32[]{:S(2)}) collective-permute-start(f32[4,512]{1,0:T(4,128)S(1)} %pad_maximum_fusion.refs_4_), channel_id=1, source_target_pairs={{8,0},{16,8},{24,16},{0,24},{9,1},{17,9},{25,17},{1,25},{10,2},{18... | collective-permute-start | bytes 24584 | tf_op jit(solution)/shard_map/ppermute | solution.py:356
  76.6 7.8 %collective-permute-start.7 = (f32[4,512]{1,0:T(4,128)S(1)}, f32[4,512]{1,0:T(4,128)S(1)}, u32[]{:S(2)}, u32[]{:S(2)}) collective-permute-start(f32[4,512]{1,0:T(4,128)S(1)} %pad_maximum_fusion.refs_4_), channel_id=1, source_target_pairs={{16,0},{24,8},{0,16},{8,24},{17,1},{25,9},{1,17},{9,25},{18,2},{26... | collective-permute-start | bytes 24584 | tf_op jit(solution)/shard_map/ppermute | solution.py:356
  78.1 6.4 %collective-permute-start.8 = (f32[4,512]{1,0:T(4,128)S(1)}, f32[4,512]{1,0:T(4,128)S(1)}, u32[]{:S(2)}, u32[]{:S(2)}) collective-permute-start(f32[4,512]{1,0:T(4,128)S(1)} %pad_maximum_fusion.refs_4_), channel_id=1, source_target_pairs={{24,0},{0,8},{8,16},{16,24},{25,1},{1,9},{9,17},{17,25},{26,2},{2,... | collective-permute-start | bytes 24584 | tf_op jit(solution)/shard_map/ppermute | solution.py:356
  80.5 10.6 %collective-permute-start.5 = (bf16[512,128]{1,0:T(8,128)(2,1)S(1)}, bf16[512,128]{1,0:T(8,128)(2,1)S(1)}, u32[]{:S(2)}, u32[]{:S(2)}) collective-permute-start(bf16[512,128]{1,0:T(8,128)(2,1)S(1)} %convolution_convert_fusion), channel_id=1, source_target_pairs={{0,24},{8,0},{16,8},{24,16},{1,25},{9,1},{17,9},{25,17},{2,26},{10... | collective-permute-start | bytes 393224 | tf_op jit(solution)/shard_map/ppermute | solution.py:363
  82.1 9.1 %collective-permute-start.3 = (bf16[512,128]{1,0:T(8,128)(2,1)S(1)}, bf16[512,128]{1,0:T(8,128)(2,1)S(1)}, u32[]{:S(2)}, u32[]{:S(2)}) collective-permute-start(bf16[512,128]{1,0:T(8,128)(2,1)S(1)} %convolution_convert_fusion.1), channel_id=1, source_target_pairs={{0,16},{8,24},{16,0},{24,8},{1,17},{9,25},{17,1},{25,9},{2,18},{10... | collective-permute-start | bytes 393224 | tf_op jit(solution)/shard_map/ppermute | solution.py:363
  83.2 4.6 %copy-start.2 = (f32[1024,512]{1,0:T(8,128)S(1)}, f32[1024,512]{1,0:T(8,128)}, u32[]{:S(2)}) copy-start(f32[1024,512]{1,0:T(8,128)} %copy-done.1) | copy-start | bytes 6291460
  83.2 4.6 %copy-start.10 = (f32[512,128]{1,0:T(8,128)S(1)}, f32[512,128]{1,0:T(8,128)}, u32[]{:S(2)}) copy-start(f32[512,128]{1,0:T(8,128)} %refs_5_.1) | copy-start | bytes 786436
  83.2 8.0 %collective-permute-start.1 = (bf16[512,128]{1,0:T(8,128)(2,1)S(1)}, bf16[512,128]{1,0:T(8,128)(2,1)S(1)}, u32[]{:S(2)}, u32[]{:S(2)}) collective-permute-start(bf16[512,128]{1,0:T(8,128)(2,1)S(1)} %convolution_convert_fusion.2), channel_id=1, source_target_pairs={{0,8},{8,16},{16,24},{24,0},{1,9},{9,17},{17,25},{25,1},{2,10},{10... | collective-permute-start | bytes 393224 | tf_op jit(solution)/shard_map/ppermute | solution.py:363
  87.8 3.4 %copy-start.8 = (s32[1,1536]{1,0:T(1,128)S(1)}, s32[1,1536]{1,0:T(1,128)}, u32[]{:S(2)}) copy-start(s32[1,1536]{1,0:T(1,128)} %refs_13_.1) | copy-start | bytes 18436
  94.6 38.2 %copy-start.6 = (f32[8192]{0:T(1024)S(1)}, f32[8192]{0:T(1024)}, u32[]{:S(2)}) copy-start(f32[8192]{0:T(1024)} %param.9) | copy-start | bytes 98308
  128.9 18.8 %all-to-all-start.3 = ((bf16[32,64,128]{2,1,0:T(8,128)(2,1)}), bf16[32,64,128]{2,1,0:T(8,128)(2,1)S(1)}, u32[]{:S(2)}, u32[]{:S(2)}) async-start(bf16[32,64,128]{2,1,0:T(8,128)(2,1)} %broadcast_in_dim.2), calls=%async_computation.3 | async-start | bytes 1048576 | tf_op jit(solution)/shard_map/all_to_all | solution.py:350
  132.8 2.2 %copy-start = (f32[8192,128]{1,0:T(8,128)S(1)}, f32[8192,128]{1,0:T(8,128)}, u32[]{:S(2)}) copy-start(f32[8192,128]{1,0:T(8,128)} %table.1) | copy-start | bytes 12582916
  147.8 0.8 copy-start.11
